TPU v7x, 768 devices: a whole 4x8x12 slice. The times are simulated.
768 devices in a mesh: section: 16 (over x, y_hi), seq: 24 (over z, y_lo), dp: 2 (over core).
Axes of the slice: x: 4, y: 8 (y_hi: 4, y_lo: 2; y = y_hi * 2 + y_lo), z: 12, core: 2. Of those that a mesh axis runs over, the one named last changes fastest.
Arguments:
- queries: bfloat16 [32, 3072, 1280], P(('section', 'dp'), 'seq'), may hold values from -5 to 5, as said below
- key_input: bfloat16 [32, 3072, 1280], P(('section', 'dp'), 'seq'), may hold values from -5 to 5
- value_input: bfloat16 [32, 3072, 1280], P(('section', 'dp'), 'seq'), may hold values from -6 to 6
- residual: bfloat16 [32, 3072, 1280], P(('section', 'dp'), 'seq'), may hold values from -4 to 4
- segments: int32 [32, 3072], P(('section', 'dp')), may hold values from 0 to 35, never falling along the last dimension, each value on 1 to 256 neighbouring positions
- out_weight: bfloat16 [1280, 1280], replicated, may hold values from -0.15625 to 0.15625
- cotangent: bfloat16 [32, 3072, 1280], P(('section', 'dp'), 'seq'), may hold values from -6 to 6
Outputs:
- mixed_out: bfloat16 [32, 3072, 1280], P(('section', 'dp'), 'seq')
- weight_grad: float32 [1280, 1280], P(('section', 'dp'))
Inputs may be any that keep to these rules, and one draw needn't show every extreme that they name: queries and key_input lie within -5 to 5.
All inputs are finite; a program needn't handle non-finite values.
Results may differ from a plain program's by a relative error of at most 0.015.
Values may be sent and summed in bfloat16 or wider, within the bound.
No kernel may reach another device: no remote copies, remote signals or barrier semaphores. Data moves between devices by JAX's collectives and lax.ppermute only.
A program may use at most 32 MiB of HBM per device.

v0:
```python
import jax
import jax.numpy as jnp
from jax import lax
from jax.sharding import PartitionSpec as P

HEADS = 16


def passed_along(value, axis, steps):
    count = lax.axis_size(axis)
    leading, last = (max(0, -steps), min(count, count - steps))
    return lax.ppermute(value, axis, [(source, source + steps) for source in range(leading, last)])


def per_device(queries, key_input, value_input, residual, segments, out_weight, cotangent):
    row_count = queries.shape[1]
    feature_width = queries.shape[2]
    head_dim = feature_width // HEADS
    my_index = lax.axis_index("seq")
    total_len = segments.shape[1]
    stacked = jnp.stack([key_input[0], value_input[0]])
    pieces = []
    offsets = []
    pieces.append(stacked)
    offsets.append(my_index * row_count)
    for distance in (1, 2, -1, -2):
        pieces.append(passed_along(stacked, "seq", distance))
        offsets.append((my_index - distance) * row_count)
    gathered = jnp.concatenate(pieces, axis=1)
    key_pos = jnp.concatenate(
        [
            offset + jnp.arange(piece.shape[1], dtype=jnp.int32)
            for offset, piece in zip(offsets, pieces)
        ]
    )
    inside = (key_pos >= 0) & (key_pos < total_len)
    key_ids = jnp.take(segments[0], jnp.clip(key_pos, 0, total_len - 1))
    query_ids = lax.dynamic_slice_in_dim(segments[0], my_index * row_count, row_count, 0)
    usable = inside[None, :] & (key_ids[None, :] == query_ids[:, None])
    key_total = gathered.shape[1]
    query_heads = queries[0].reshape(row_count, HEADS, head_dim)
    key_heads = gathered[0].reshape(key_total, HEADS, head_dim)
    value_heads = gathered[1].reshape(key_total, HEADS, head_dim)
    scores = jnp.einsum(
        "qhd,khd->hqk", query_heads, key_heads, preferred_element_type=jnp.float32
    ) * head_dim ** (-0.5)
    scores = jnp.where(usable[None], scores, jnp.float32(-1e30))
    highest = jnp.max(scores, axis=-1, keepdims=True)
    expo = jnp.where(usable[None], jnp.exp(scores - highest), jnp.float32(0.0))
    probs = (expo / jnp.sum(expo, axis=-1, keepdims=True)).astype(jnp.bfloat16)
    attended = jnp.einsum("hqk,khd->qhd", probs, value_heads, preferred_element_type=jnp.float32)
    attended = attended.reshape(row_count, feature_width).astype(jnp.bfloat16)
    projected = lax.dot_general(
        attended, out_weight, (((1,), (1,)), ((), ())), preferred_element_type=jnp.float32
    )
    mixed_out = (residual[0].astype(jnp.float32) + projected).astype(jnp.bfloat16)[None]
    groups = lax.axis_size("section") * lax.axis_size("dp")
    grad_scale = 1.0 / float(groups * total_len) ** 0.5
    grad_input = cotangent[0]
    partial_value = (
        lax.dot_general(
            grad_input, attended, (((0,), (0,)), ((), ())), preferred_element_type=jnp.float32
        )
        * grad_scale
    )
    reduced = lax.psum_scatter(
        partial_value.astype(jnp.bfloat16), ("section", "dp"), scatter_dimension=0, tiled=True
    ).astype(jnp.float32)
    weight_grad = lax.psum(reduced, "seq")
    return (mixed_out, weight_grad)


def solution(mesh):
    in_specs = (
        P(("section", "dp"), "seq", None),
        P(("section", "dp"), "seq", None),
        P(("section", "dp"), "seq", None),
        P(("section", "dp"), "seq", None),
        P(("section", "dp"), None),
        P(),
        P(("section", "dp"), "seq", None),
    )
    out_specs = (P(("section", "dp"), "seq", None), P(("section", "dp"), None))
    return jax.shard_map(
        per_device, mesh=mesh, in_specs=in_specs, out_specs=out_specs, check_vma=False
    )
```

profile of v0, /device:TPU:20, one launch (start us, length us, event | category | flops | bytes accessed | tf_op | source)
XLA Modules:
  0.0 313.1 jit_solution(9306173479509987143)
XLA Ops:
  7.2 0.0 copy-start
  7.2 0.0 reduce-scatter.4.cloned.1.call-start
  7.2 2.0 constant_dynamic-update-slice_fusion.1
  9.2 1.9 constant_dynamic-update-slice_fusion
  11.1 4.3 %collective-permute-start = (bf16[2,128,1280]{2,1,0:T(8,128)(2,1)}, bf16[2,128,1280]{2,1,0:T(8,128)(2,1)}, u32[]{:S(2)}, u32[]{:S(2)}) collective-permute-start(bf16[2,128,1280]{2,1,0:T(8,128)(2,1)} %get-tuple-element.10), channel_id=1, source_target_pairs={{0,2},{2,4},{4,6},{6,8},{8,10},{10,12},{12,14},{14,16},{16,18},{18... | collective-permute-start | bytes 1966088 | tf_op jit(solution)/shard_map/ppermute | solution.py:12
  15.4 4.3 %collective-permute-start.1 = (bf16[2,128,1280]{2,1,0:T(8,128)(2,1)}, bf16[2,128,1280]{2,1,0:T(8,128)(2,1)}, u32[]{:S(2)}, u32[]{:S(2)}) collective-permute-start(bf16[2,128,1280]{2,1,0:T(8,128)(2,1)} %get-tuple-element.10), channel_id=1, source_target_pairs={{0,4},{2,6},{4,8},{6,10},{8,12},{10,14},{12,16},{14,18},{16,20},{1... | collective-permute-start | bytes 1966088 | tf_op jit(solution)/shard_map/ppermute | solution.py:12
  19.7 1.3 collective-permute-start.2
  21.0 1.3 collective-permute-start.3
  22.5 1.9 copy.21
  24.4 0.7 dynamic-slice_bitcast_fusion
  25.0 3.9 %gather_fusion = s32[640]{0:T(1024)S(1)} fusion(s32[3072]{0:T(1024)S(1)} %bitcast.49, s32[1024]{0:T(1024)S(1)} %pad_clamp_fusion), kind=kCustom, calls=%fused_computation | custom fusion | bytes 7680 | tf_op jit(solution)/shard_map/jit(_take)/gather | solution.py:37
  28.9 0.2 compare_and_fusion
  29.2 13.7 %collective-permute-done = bf16[2,128,1280]{2,1,0:T(8,128)(2,1)} collective-permute-done((bf16[2,128,1280]{2,1,0:T(8,128)(2,1)}, bf16[2,128,1280]{2,1,0:T(8,128)(2,1)}, u32[]{:S(2)}, u32[]{:S(2)}) %collective-permute-start) | collective-permute-done | bytes 655392 | tf_op jit(solution)/shard_map/ppermute | solution.py:12
  42.9 2.0 constant_dynamic-update-slice_fusion.5
  44.9 2.0 constant_dynamic-update-slice_fusion.4
  46.9 2.0 constant_dynamic-update-slice_fusion.3
  48.9 4.8 %collective-permute-done.3 = bf16[2,128,1280]{2,1,0:T(8,128)(2,1)} collective-permute-done((bf16[2,128,1280]{2,1,0:T(8,128)(2,1)}, bf16[2,128,1280]{2,1,0:T(8,128)(2,1)}, u32[]{:S(2)}, u32[]{:S(2)}) %collective-permute-start.3) | collective-permute-done | bytes 655392 | tf_op jit(solution)/shard_map/ppermute | solution.py:12
  53.6 2.0 constant_dynamic-update-slice_fusion.2
  55.6 3.8 %fusion.17 = (bf16[1,640,1280]{2,1,0:T(8,128)(2,1)}, bf16[1,640,1280]{2,1,0:T(8,128)(2,1)}) fusion(bf16[2,640,1280]{2,1,0:T(8,128)(2,1)} %constant_dynamic-update-slice_fusion.2), kind=kLoop, calls=%fused_computation.52 | loop fusion | bytes 6553600 | tf_op jit(solution)/shard_map/slice | solution.py:42
  59.4 3.5 %copy.19 = bf16[1,640,1280]{1,2,0:T(8,128)(2,1)} copy(bf16[1,640,1280]{2,1,0:T(8,128)(2,1)} %get-tuple-element.9) | data formatting | bytes 3276800 | tf_op jit(solution)/shard_map/slice | solution.py:43
  62.9 3.6 %copy.20 = bf16[1,640,1280]{1,2,0:T(8,128)(2,1)} copy(bf16[1,640,1280]{2,1,0:T(8,128)(2,1)} %get-tuple-element.8) | data formatting | bytes 3276800 | tf_op jit(solution)/shard_map/slice | solution.py:42
  66.5 6.1 %fusion.18 = (f32[16,128]{1,0:T(8,128)S(1)}, f32[16,128,640]{1,2,0:T(8,128)}) fusion(pred[128,640]{0,1:T(8,128)(4,1)S(1)} %compare_and_fusion, bf16[640,16,80]{0,2,1:T(8,128)(2,1)} %bitcast.51, bf16[128,16,80]{0,2,1:T(8,128)(2,1)} %bitcast.54), kind=kOutput, calls=%fused_computation.53 | convolution fusion | flops 216269440 | bytes 7299072 | tf_op jit(solution)/shard_map/sub | solution.py:49
  72.6 3.7 %fusion.10 = bf16[16,80,128]{2,1,0:T(8,128)(2,1)S(1)} fusion(bf16[640,16,80]{0,2,1:T(8,128)(2,1)} %bitcast.50, f32[16,128,640]{1,2,0:T(8,128)} %get-tuple-element.15, f32[16,128]{1,0:T(8,128)S(1)} %get-tuple-element.14), kind=kOutput, calls=%fused_computation.16 | convolution fusion | flops 212500480 | bytes 7217152 | tf_op jit(solution)/shard_map/hqk,khd->qhd/dot_general | solution.py:51
  76.3 0.7 copy-done.2
  77.0 2.7 fusion.2
  79.8 5.6 %copy.25 = bf16[1280,1280]{1,0:T(8,128)(2,1)} copy(bf16[1280,1280]{0,1:T(8,128)(2,1)} %fusion.2) | data formatting | bytes 6553600
  85.4 0.0 reduce-scatter.4.cloned.1.call-update
  85.4 3.0 fusion.9
  88.4 111.5 %reduce-scatter.4.cloned.1.call-done = bf16[40,1280]{1,0:T(8,128)(2,1)} async-done(((bf16[1280,1280]{1,0:T(8,128)(2,1)}), bf16[40,1280]{1,0:T(8,128)(2,1)}) %reduce-scatter.4.cloned.1.call-update) | async-done | bytes 102416
  199.9 1.8 copy.26
  201.7 102.6 %all-reduce.1 = f32[40,1280]{0,1:T(8,128)} all-reduce(bf16[40,1280]{0,1:T(8,128)(2,1)} %copy.26), channel_id=1, replica_groups=mesh['section'=16,'seq'=24,'dp'=2] {'seq'}, use_global_device_ids=true, to_apply=%region_3.4 | all-reduce | flops 51200 | bytes 307200 | tf_op jit(solution)/shard_map/psum | solution.py:69
  304.3 2.0 copy.23
  (23 shorter events, 0.1 us)
Async XLA Ops:
  7.2 78.3 %copy-start = (bf16[1280,1280]{1,0:T(8,128)(2,1)S(1)}, bf16[1280,1280]{1,0:T(8,128)(2,1)}, u32[]{:S(2)}) copy-start(bf16[1280,1280]{1,0:T(8,128)(2,1)} %param.12) | copy-start | bytes 9830404
  7.2 17.9 %copy-start.1 = (s32[1,3072]{1,0:T(1,128)S(1)}, s32[1,3072]{1,0:T(1,128)}, u32[]{:S(2)}) copy-start(s32[1,3072]{1,0:T(1,128)} %param.11) | copy-start | bytes 36868
  7.2 192.7 %reduce-scatter.4.cloned.1.call-start = ((), (), s32[]{:S(2)}) async-start(), calls=%async_computation.1 | async-start | bytes 3379200
  11.1 31.8 %collective-permute-start = (bf16[2,128,1280]{2,1,0:T(8,128)(2,1)}, bf16[2,128,1280]{2,1,0:T(8,128)(2,1)}, u32[]{:S(2)}, u32[]{:S(2)}) collective-permute-start(bf16[2,128,1280]{2,1,0:T(8,128)(2,1)} %get-tuple-element.10), channel_id=1, source_target_pairs={{0,2},{2,4},{4,6},{6,8},{8,10},{10,12},{12,14},{14,16},{16,18},{18... | collective-permute-start | bytes 1966088 | tf_op jit(solution)/shard_map/ppermute | solution.py:12
  15.4 29.5 %collective-permute-start.1 = (bf16[2,128,1280]{2,1,0:T(8,128)(2,1)}, bf16[2,128,1280]{2,1,0:T(8,128)(2,1)}, u32[]{:S(2)}, u32[]{:S(2)}) collective-permute-start(bf16[2,128,1280]{2,1,0:T(8,128)(2,1)} %get-tuple-element.10), channel_id=1, source_target_pairs={{0,4},{2,6},{4,8},{6,10},{8,12},{10,14},{12,16},{14,18},{16,20},{1... | collective-permute-start | bytes 1966088 | tf_op jit(solution)/shard_map/ppermute | solution.py:12
  19.7 27.2 %collective-permute-start.2 = (bf16[2,128,1280]{2,1,0:T(8,128)(2,1)}, bf16[2,128,1280]{2,1,0:T(8,128)(2,1)}, u32[]{:S(2)}, u32[]{:S(2)}) collective-permute-start(bf16[2,128,1280]{2,1,0:T(8,128)(2,1)} %get-tuple-element.10), channel_id=1, source_target_pairs={{2,0},{4,2},{6,4},{8,6},{10,8},{12,10},{14,12},{16,14},{18,16},{20... | collective-permute-start | bytes 1966088 | tf_op jit(solution)/shard_map/ppermute | solution.py:12
  21.0 32.6 %collective-permute-start.3 = (bf16[2,128,1280]{2,1,0:T(8,128)(2,1)}, bf16[2,128,1280]{2,1,0:T(8,128)(2,1)}, u32[]{:S(2)}, u32[]{:S(2)}) collective-permute-start(bf16[2,128,1280]{2,1,0:T(8,128)(2,1)} %get-tuple-element.10), channel_id=1, source_target_pairs={{4,0},{6,2},{8,4},{10,6},{12,8},{14,10},{16,12},{18,14},{20,16},{2... | collective-permute-start | bytes 1966088 | tf_op jit(solution)/shard_map/ppermute | solution.py:12
  72.6 4.5 %copy-start.3 = (bf16[1,128,1280]{2,1,0:T(8,128)(2,1)S(1)}, bf16[1,128,1280]{2,1,0:T(8,128)(2,1)}, u32[]{:S(2)}) copy-start(bf16[1,128,1280]{2,1,0:T(8,128)(2,1)} %param.13) | copy-start | bytes 983044
  76.3 0.7 copy-start.2
Sparse Core Ops, SparseCore 0:
  85.5 114.3 reduce-scatter.3
where the time goes:
time: 314 us; the launch traced here: 313 us
  waiting for transfers between devices  130 us (41%)
  blocking collectives  103 us (33%)
  local copies, waits for them, and re-layouts  39.2 us (12%)
  matrix products  15.5 us (5%)
  between operations  14.2 us (5%)
  starting transfers between devices  11.2 us (4%)
    unnamed x2, waiting for transfers between devices  112 us
    psum x1, blocking collectives, per_device(): weight_grad = lax.psum(reduced, 'seq')  103 us
    unnamed x16, local copies, waits for them, and re-layouts  20 us
    ppermute x4, waiting for transfers between devices, passed_along(): lax.ppermute(value, axis, [(source, source + steps) for source in range(l...  18.5 us
    ppermute x4, starting transfers between devices, passed_along(): lax.ppermute(value, axis, [(source, source + steps) for source in range(l...  11.2 us
    slice x2, local copies, waits for them, and re-layouts, per_device(): key_heads = gathered[0].reshape(key_total, HEADS, head_dim)  7.38 us
  transfers between devices with their start and end apart: 5, of which 3 were waited for; matrix products, arithmetic and copies ran while one was open for 5% of the time, Pallas kernels for 0%

commit v1 on v0

v1 whole, which is shorter than its diff:
```python
import functools

import jax
import jax.numpy as jnp
from jax import lax
from jax.experimental import pallas as pl
from jax.experimental.pallas import tpu as pltpu
from jax.sharding import PartitionSpec as P


HEADS = 16
LOG2E = 1.4426950408889634
AXES = ("section", "seq", "dp")
ANY = pl.BlockSpec(memory_space=pl.ANY)
VMEM = pl.BlockSpec(memory_space=pltpu.VMEM)
SMEM = pl.BlockSpec(memory_space=pltpu.SMEM)
NT = (((1,), (1,)), ((), ()))


def moved(value, target):
    sections, seqs, cores = (lax.axis_size(axis) for axis in AXES)
    pairs = []
    for section in range(sections):
        for seq in range(seqs):
            for core in range(cores):
                to_seq, to_core = target(seq, core)
                if 0 <= to_seq < seqs:
                    source = (section * seqs + seq) * cores + core
                    pairs.append((source, (section * seqs + to_seq) * cores + to_core))
    return lax.ppermute(value, AXES, pairs)


def to_pair(value):
    return moved(value, lambda seq, core: (seq ^ 1, core))


def to_core(value):
    return moved(value, lambda seq, core: (seq, 1 - core))


def to_next(value):
    return moved(value, lambda seq, core: (seq + 2, core))


def to_previous(value):
    return moved(value, lambda seq, core: (seq - 2, core))


def position(place):
    index = place[0]
    return index >> 2, (index >> 1) & 1, index & 1


def split_kernel(
    width, place, query, key, value, cotangent, kv_own, kv_other, q_own, q_other, exchanged
):
    _, y, _ = position(place)
    half = q_own.shape[1]
    own = pl.ds(pl.multiple_of(y * half, half), half)
    other = pl.ds(pl.multiple_of((1 - y) * half, half), half)
    kv_own[0] = key[:, own]
    kv_own[1] = value[:, own]
    kv_other[0] = key[:, other]
    kv_other[1] = value[:, other]
    q_own[...] = query[:, own]
    q_other[...] = query[:, other]
    picked = half // 2
    shift = 20
    factor = -(-(1 << shift) // width)
    assert all((j * factor) >> shift == j // width for j in range(picked))
    row = lax.broadcasted_iota(jnp.int32, (picked, half), 0)
    column = lax.broadcasted_iota(jnp.int32, (picked, half), 1)
    base = row + lax.shift_right_logical(row * factor, shift) * width
    for to_core_index in range(2):
        chosen = (column == base + to_core_index * width).astype(jnp.float32)
        chosen = chosen.astype(jnp.bfloat16)
        parts = [
            lax.dot_general(
                cotangent[:, part * half : (part + 1) * half],
                chosen,
                NT,
                preferred_element_type=jnp.float32,
            )
            for part in range(2)
        ]
        block = jnp.concatenate(parts, axis=1).astype(jnp.bfloat16)
        for side in range(2):
            exchanged[side * 2 + to_core_index] = block


def attention_kernel(
    head_dim, place, segments, q_own, q_pair, kv_own, kv_pair, kv_left, kv_left_pair,
    kv_right, kv_right_pair, attended, passed, queries, keys, values, bias, mixed, sems
):
    rows, half = q_own.shape
    total = segments.shape[1]
    z, y, _ = position(place)
    blocks = (kv_own, kv_pair, kv_left, kv_left_pair, kv_right, kv_right_pair)
    copies = [
        pltpu.make_async_copy(q_own, queries.at[pl.ds(0, rows)], sems.at[0]),
        pltpu.make_async_copy(q_pair, queries.at[pl.ds(rows, rows)], sems.at[1]),
    ]
    for i, block in enumerate(blocks):
        here = pl.ds(i * rows, rows)
        copies.append(pltpu.make_async_copy(block.at[0], keys.at[here], sems.at[2 + 2 * i]))
        copies.append(pltpu.make_async_copy(block.at[1], values.at[here], sems.at[3 + 2 * i]))
    for copy in copies:
        copy.start()
    ids = []
    for unit in (0, -1, 1):
        for side in (y, 1 - y):
            offset = ((z + unit) * 2 + side) * rows
            start = pl.multiple_of(jnp.clip(offset, 0, total - rows), rows)
            row = segments[:, pl.ds(start, rows)]
            ids.append(jnp.where((offset >= 0) & (offset < total), row, -1))
    for i in range(2):
        query_ids = jnp.transpose(jnp.broadcast_to(ids[i], (rows, rows)))
        for j in range(6):
            bias[i * rows : (i + 1) * rows, j * rows : (j + 1) * rows] = jnp.where(
                query_ids == ids[j], jnp.float32(0.0), jnp.float32(-1e30)
            )
    mixed[...] = jnp.zeros_like(mixed)
    for copy in copies:
        copy.wait()
    scale = head_dim ** (-0.5) * LOG2E
    for i in range(2):
        here = slice(i * rows, (i + 1) * rows)
        for head in range(half // head_dim):
            first, last = head * head_dim, (head + 1) * head_dim
            low, high = first // 128 * 128, -(-last // 128) * 128
            lane = lax.broadcasted_iota(jnp.int32, (rows, high - low), 1) + low
            inside = (lane >= first) & (lane < last)
            query = jnp.where(inside, queries[here, low:high], jnp.zeros((), jnp.bfloat16))
            scores = lax.dot_general(
                query, keys[:, low:high], NT, preferred_element_type=jnp.float32
            )
            scores = scores + bias[here, :]
            highest = jnp.max(scores, axis=-1, keepdims=True)
            expo = jnp.exp2((scores - highest) * scale)
            norm = 1.0 / jnp.sum(expo, axis=-1, keepdims=True)
            weighted = jnp.dot(
                expo.astype(jnp.bfloat16), values[:, low:high], preferred_element_type=jnp.float32
            )
            mixed[here, low:high] = jnp.where(inside, weighted * norm, mixed[here, low:high])
    attended[...] = mixed[...].astype(jnp.bfloat16)
    passed[...] = mixed[rows:, :].astype(jnp.bfloat16)


def gradient_kernel(share, width, place, att, att_core, exchanged, out):
    _, y, core = position(place)
    order = (2 * y + core, 2 * (1 - y) + core, 2 * y + 1 - core, 2 * (1 - y) + 1 - core)
    left = jnp.concatenate([exchanged[index] for index in order], axis=0)
    right = jnp.concatenate([att[...], att_core[...]], axis=0)
    full = lax.dot_general(
        left, right, (((0,), (0,)), ((), ())), preferred_element_type=jnp.float32
    )
    wide = full.shape[1] // 128
    parts = out.shape[0] // (full.shape[0] // width)
    for section in range(full.shape[0] // width):
        for part in range(parts):
            for slot in range(share):
                row, column = divmod(part * share + slot, wide)
                if row * 8 < width:
                    row = section * width + row * 8
                    tile = full[row : row + 8, column * 128 : (column + 1) * 128]
                else:
                    tile = jnp.zeros((8, 128), jnp.float32)
                out[section * parts + part, slot * 8 : (slot + 1) * 8, :] = tile.astype(
                    jnp.bfloat16
                )


def total_kernel(scale, terms, out):
    total = jnp.sum(terms[...].astype(jnp.float32), axis=0) * scale
    total = total.astype(jnp.bfloat16)
    for i in range(out.shape[0]):
        out[i] = total


def assembly_kernel(share, parts, terms, out):
    groups = terms.shape[0] // (2 * parts)
    wide = out.shape[1] // 256
    for side in range(2):
        for tile in range(out.shape[0] // 8 * wide):
            row, column = divmod(tile, wide)
            part, slot = divmod(tile, share)
            total = sum(
                terms[(group * parts + part) * 2 + side, slot * 8 : (slot + 1) * 8, :].astype(
                    jnp.float32
                )
                for group in range(groups)
            )
            column = (side * wide + column) * 128
            out[row * 8 : (row + 1) * 8, column : column + 128] = total


def projection_kernel(place, attended, received, weight, residual, out):
    rows, half = received.shape
    _, y, _ = position(place)
    own = pl.ds(pl.multiple_of(y * half, half), half)
    other = pl.ds(pl.multiple_of((1 - y) * half, half), half)
    total = lax.dot_general(
        attended[:rows, :], weight[:, own], NT, preferred_element_type=jnp.float32
    )
    total += lax.dot_general(
        received[...], weight[:, other], NT, preferred_element_type=jnp.float32
    )
    out[...] = (residual[...].astype(jnp.float32) + total).astype(jnp.bfloat16)


def call(kernel, outs, in_specs, flops, moved_bytes, scratch=(), grant=16):
    return pl.pallas_call(
        kernel,
        out_shape=outs,
        in_specs=in_specs,
        out_specs=jax.tree.map(lambda _: VMEM, outs),
        scratch_shapes=scratch,
        cost_estimate=pl.CostEstimate(
            flops=flops, bytes_accessed=moved_bytes, transcendentals=0
        ),
        compiler_params=pltpu.CompilerParams(vmem_limit_bytes=grant << 20),
    )


def per_device(queries, key_input, value_input, residual, segments, out_weight, cotangent):
    rows, features = queries.shape[1], queries.shape[2]
    half = features // 2
    head_dim = features // HEADS
    sections, seqs, cores = (lax.axis_size(axis) for axis in AXES)
    units = seqs // 2
    width = features // (sections * cores)
    place = lax.axis_index(("seq", "dp")).astype(jnp.int32).reshape(1)

    def bf16(*shape):
        return jax.ShapeDtypeStruct(shape, jnp.bfloat16)

    kv_own, kv_other, q_own, q_other, exchanged = call(
        functools.partial(split_kernel, width),
        (
            bf16(2, rows, half),
            bf16(2, rows, half),
            bf16(rows, half),
            bf16(rows, half),
            bf16(4, rows, half),
        ),
        [SMEM, VMEM, VMEM, VMEM, VMEM],
        2 * half * features * rows,
        24 * rows * features,
        grant=62,
    )(place, queries[0], key_input[0], value_input[0], cotangent[0])
    kv_pair = to_pair(kv_other)
    kv_left = to_next(kv_own)
    kv_right = to_previous(kv_own)
    kv_left_pair = to_next(kv_pair)
    kv_right_pair = to_previous(kv_pair)
    q_pair = to_pair(q_other)
    quads = [list(range(first, first + 4)) for first in range(0, 2 * seqs, 4)]
    exchanged = lax.all_to_all(exchanged, ("seq", "dp"), 0, 0, tiled=True, axis_index_groups=quads)
    attended, passed = call(
        functools.partial(attention_kernel, head_dim),
        (bf16(2 * rows, half), bf16(rows, half)),
        [SMEM, VMEM] + [ANY] * 8,
        4 * 2 * rows * 6 * rows * half,
        26 * rows * half,
        scratch=[
            pltpu.VMEM((2 * rows, half), jnp.bfloat16),
            pltpu.VMEM((6 * rows, half), jnp.bfloat16),
            pltpu.VMEM((6 * rows, half), jnp.bfloat16),
            pltpu.VMEM((2 * rows, 6 * rows), jnp.float32),
            pltpu.VMEM((2 * rows, half), jnp.float32),
            pltpu.SemaphoreType.DMA((14,)),
        ],
    )(
        place, segments, q_own, q_pair, kv_own, kv_pair, kv_left, kv_left_pair,
        kv_right, kv_right_pair,
    )
    attended_core = to_core(attended)
    received = to_pair(passed)
    parts = 4 if units % 4 == 0 else 2
    tiles = width // 8 * (half // 128)
    share = -(-tiles // parts)
    partial = call(
        functools.partial(gradient_kernel, share, width),
        bf16(sections * parts, share * 8, 128),
        [SMEM, VMEM, VMEM, VMEM],
        2 * half * half * 4 * rows,
        2 * half * half,
    )(place, attended, attended_core, exchanged)
    mixed_out = call(
        projection_kernel,
        bf16(rows, features),
        [SMEM] + [VMEM] * 4,
        2 * rows * features * features,
        2 * features * features,
    )(place, attended, received, out_weight, residual[0])

    groups = sections * cores
    grad_scale = 1.0 / float(groups * seqs * rows) ** 0.5
    cubes = [
        [
            (section * seqs + (first + part) * 2 + side) * cores + core
            for section in range(sections)
            for part in range(parts)
        ]
        for first in range(0, units, parts)
        for side in range(2)
        for core in range(cores)
    ]
    terms = lax.all_to_all(partial, AXES, 0, 0, tiled=True, axis_index_groups=cubes)
    spread = call(
        functools.partial(total_kernel, grad_scale),
        bf16(seqs, share * 8, 128),
        [VMEM],
        sections * parts * share * 1024,
        2 * (sections * parts + seqs) * share * 1024,
    )(terms)
    spread = lax.all_to_all(spread, "seq", 0, 0, tiled=True)
    weight_grad = call(
        functools.partial(assembly_kernel, share, parts),
        jax.ShapeDtypeStruct((width, features), jnp.float32),
        [VMEM],
        seqs * share * 1024,
        2 * seqs * share * 1024,
    )(spread)
    return (mixed_out[None], weight_grad)


def solution(mesh):
    in_specs = (
        P(("section", "dp"), "seq", None),
        P(("section", "dp"), "seq", None),
        P(("section", "dp"), "seq", None),
        P(("section", "dp"), "seq", None),
        P(("section", "dp"), None),
        P(),
        P(("section", "dp"), "seq", None),
    )
    out_specs = (P(("section", "dp"), "seq", None), P(("section", "dp"), None))
    return jax.shard_map(
        per_device, mesh=mesh, in_specs=in_specs, out_specs=out_specs, check_vma=False
    )
```

time: 314 us -> 128 us (0.41)
  the two profiles are of different devices: /device:TPU:20 before, /device:TPU:8 now
where the time goes in v1:
time: 128 us
  starting transfers between devices  45.3 us (35%)
  blocking collectives  39 us (30%)
  waiting for transfers between devices  19.2 us (15%)
  Pallas kernels  19.1 us (15%)
  local copies, waits for them, and re-layouts  4.3 us (3%)
    all_to_all x1, blocking collectives, per_device(): lax.all_to_all(partial, AXES, 0, 0, tiled=True, axis_index_groups=cubes)  39 us
    ppermute x8, starting transfers between devices, moved(): return lax.ppermute(value, AXES, pairs)  29.3 us
    ppermute x8, waiting for transfers between devices, moved(): return lax.ppermute(value, AXES, pairs)  13.7 us
    all_to_all x1, starting transfers between devices, per_device(): spread = lax.all_to_all(spread, 'seq', 0, 0, tiled=True)  11.8 us
    pallas_call x1, Pallas kernels, per_device(): call(functools.partial(attention_kernel, head_dim), (bf16(2 * rows, half)...  9.2 us
    all_to_all x1, waiting for transfers between devices, per_device(): spread = lax.all_to_all(spread, 'seq', 0, 0, tiled=True)  5.43 us
    unnamed x12, local copies, waits for them, and re-layouts  4.3 us
    all_to_all x1, starting transfers between devices, per_device(): lax.all_to_all(exchanged, ('seq', 'dp'), 0, 0, tiled=True, axis_index_gro...  4.16 us
  transfers between devices with their start and end apart: 10, of which 5 were waited for; matrix products, arithmetic and copies ran while one was open for 0% of the time, Pallas kernels for 9%

profile of v1, /device:TPU:8, one launch (start us, length us, event | category | flops | bytes accessed | tf_op | source)
XLA Modules:
  0.0 127.6 jit_solution(5312984933745223833)
XLA Ops:
  0.6 3.2 %shard_map.86 = (bf16[2,128,640]{2,1,0:T(8,128)(2,1)}, bf16[2,128,640]{2,1,0:T(8,128)(2,1)}, bf16[128,640]{1,0:T(8,128)(2,1)}, bf16[128,640]{1,0:T(8,128)(2,1)}, bf16[4,128,640]{2,1,0:T(8,128)(2,1)}) custom-call(s32[1]{0:T(128)} %bitcast.place, bf16[128,1280]{1,0:T(8,128)(2,1)} %bitcast.9, bf16[128,1280]{1,0:T(8,128)(2,1)} %bitcast.10, ...), custom_call_target="tpu_custom_call" | custom-call | flops 209715200 | bytes 3932160 | tf_op jit(solution)/shard_map/pallas_call | solution.py:237
  3.8 11.3 %collective-permute-start.1 = (bf16[2,128,640]{2,1,0:T(8,128)(2,1)}, bf16[2,128,640]{2,1,0:T(8,128)(2,1)S(1)}, u32[]{:S(2)}, u32[]{:S(2)}) collective-permute-start(bf16[2,128,640]{2,1,0:T(8,128)(2,1)} %get-tuple-element.12), channel_id=1, source_target_pairs={{0,2},{1,3},{2,0},{3,1},{4,6},{5,7},{6,4},{7,5},{8,10},{9,11},{10,... | collective-permute-start | bytes 983048 | tf_op jit(solution)/shard_map/ppermute | solution.py:30
  15.2 4.2 %all-to-all-start = ((bf16[4,128,640]{2,1,0:T(8,128)(2,1)}), bf16[4,128,640]{2,1,0:T(8,128)(2,1)}, u32[]{:S(2)}, u32[]{:S(2)}) async-start(bf16[4,128,640]{2,1,0:T(8,128)(2,1)} %get-tuple-element.15), calls=%async_computation | async-start | bytes 1310720 | tf_op jit(solution)/shard_map/all_to_all | solution.py:258
  19.3 1.3 %collective-permute-start.4 = (bf16[2,128,640]{2,1,0:T(8,128)(2,1)}, bf16[2,128,640]{2,1,0:T(8,128)(2,1)S(1)}, u32[]{:S(2)}, u32[]{:S(2)}) collective-permute-start(bf16[2,128,640]{2,1,0:T(8,128)(2,1)} %get-tuple-element.11.kv_own), channel_id=1, source_target_pairs={{4,0},{5,1},{6,2},{7,3},{8,4},{9,5},{10,6},{11,7},{12,8},{13,9},{1... | collective-permute-start | bytes 983048 | tf_op jit(solution)/shard_map/ppermute | solution.py:30
  20.6 4.6 %collective-permute-start.2 = (bf16[2,128,640]{2,1,0:T(8,128)(2,1)}, bf16[2,128,640]{2,1,0:T(8,128)(2,1)S(1)}, u32[]{:S(2)}, u32[]{:S(2)}) collective-permute-start(bf16[2,128,640]{2,1,0:T(8,128)(2,1)} %get-tuple-element.11.kv_own), channel_id=1, source_target_pairs={{0,4},{1,5},{2,6},{3,7},{4,8},{5,9},{6,10},{7,11},{8,12},{9,13},{1... | collective-permute-start | bytes 983048 | tf_op jit(solution)/shard_map/ppermute | solution.py:30
  25.2 0.0 collective-permute-done.1.kv_pair
  25.2 1.3 %collective-permute-start.5 = (bf16[2,128,640]{2,1,0:T(8,128)(2,1)S(1)}, bf16[2,128,640]{2,1,0:T(8,128)(2,1)S(1)}, u32[]{:S(2)}, u32[]{:S(2)}) collective-permute-start(bf16[2,128,640]{2,1,0:T(8,128)(2,1)S(1)} %collective-permute-done.1.kv_pair), channel_id=1, source_target_pairs={{4,0},{5,1},{6,2},{7,3},{8,4},{9,5},{10,6},{11,7},{12,8},{13,9},{1... | collective-permute-start | bytes 983048 | tf_op jit(solution)/shard_map/ppermute | solution.py:30
  26.5 4.6 %collective-permute-start.3 = (bf16[2,128,640]{2,1,0:T(8,128)(2,1)S(1)}, bf16[2,128,640]{2,1,0:T(8,128)(2,1)S(1)}, u32[]{:S(2)}, u32[]{:S(2)}) collective-permute-start(bf16[2,128,640]{2,1,0:T(8,128)(2,1)S(1)} %collective-permute-done.1.kv_pair), channel_id=1, source_target_pairs={{0,4},{1,5},{2,6},{3,7},{4,8},{5,9},{6,10},{7,11},{8,12},{9,13},{1... | collective-permute-start | bytes 983048 | tf_op jit(solution)/shard_map/ppermute | solution.py:30
  31.1 1.9 %collective-permute-start = (bf16[128,640]{1,0:T(8,128)(2,1)}, bf16[128,640]{1,0:T(8,128)(2,1)S(1)}, u32[]{:S(2)}, u32[]{:S(2)}) collective-permute-start(bf16[128,640]{1,0:T(8,128)(2,1)} %get-tuple-element.10), channel_id=1, source_target_pairs={{0,2},{1,3},{2,0},{3,1},{4,6},{5,7},{6,4},{7,5},{8,10},{9,11},{10,... | collective-permute-start | bytes 491528 | tf_op jit(solution)/shard_map/ppermute | solution.py:30
  33.0 5.5 %collective-permute-done.q_pair = bf16[128,640]{1,0:T(8,128)(2,1)S(1)} collective-permute-done((bf16[128,640]{1,0:T(8,128)(2,1)}, bf16[128,640]{1,0:T(8,128)(2,1)S(1)}, u32[]{:S(2)}, u32[]{:S(2)}) %collective-permute-start) | collective-permute-done | bytes 163872 | tf_op jit(solution)/shard_map/ppermute | solution.py:30
  38.5 0.0 collective-permute-done.4.kv_right
  38.5 0.0 collective-permute-done.2.kv_left
  38.5 0.0 collective-permute-done.5.kv_right_pair
  38.5 0.8 collective-permute-done.3.kv_left_pair
  39.3 1.0 copy-done.3
  40.3 0.9 copy-done.4
  41.2 0.7 copy-done.5
  41.9 9.2 %shard_map.87 = (bf16[256,640]{1,0:T(8,128)(2,1)}, bf16[128,640]{1,0:T(8,128)(2,1)S(1)}) custom-call(s32[1]{0:T(128)} %bitcast.place, s32[1,3072]{1,0:T(1,128)S(1)} %copy-done.5, bf16[128,640]{1,0:T(8,128)(2,1)S(1)} %copy-done.4, bf16[128,640]{1,0:T(8,128)(2,1)S(1)} %collective-permute-done.q_pair, bf16[2,128,640]{2,1,0:T(8,128)(2,1)S(1)} %copy-done.3, ...), custom_call_target="tpu_custom_call" | custom-call | flops 503316480 | bytes 2129920 | tf_op jit(solution)/shard_map/pallas_call | solution.py:259
  51.1 0.0 copy-start
  51.1 2.2 %collective-permute-start.7 = (bf16[256,640]{1,0:T(8,128)(2,1)}, bf16[256,640]{1,0:T(8,128)(2,1)}, u32[]{:S(2)}, u32[]{:S(2)}) collective-permute-start(bf16[256,640]{1,0:T(8,128)(2,1)} %get-tuple-element.13.attended.att), channel_id=1, source_target_pairs={{0,1},{1,0},{2,3},{3,2},{4,5},{5,4},{6,7},{7,6},{8,9},{9,8},{10,11... | collective-permute-start | bytes 983048 | tf_op jit(solution)/shard_map/ppermute | solution.py:30
  53.3 1.9 %collective-permute-done.7.att_core = bf16[256,640]{1,0:T(8,128)(2,1)} collective-permute-done((bf16[256,640]{1,0:T(8,128)(2,1)}, bf16[256,640]{1,0:T(8,128)(2,1)}, u32[]{:S(2)}, u32[]{:S(2)}) %collective-permute-start.7) | collective-permute-done | bytes 327712 | tf_op jit(solution)/shard_map/ppermute | solution.py:30
  55.3 2.0 %shard_map.89 = bf16[64,56,128]{2,1,0:T(8,128)(2,1)S(1)} custom-call(s32[1]{0:T(128)} %bitcast.place, bf16[256,640]{1,0:T(8,128)(2,1)} %get-tuple-element.13.attended.att, bf16[256,640]{1,0:T(8,128)(2,1)} %collective-permute-done.7.att_core, bf16[4,128,640]{2,1,0:T(8,128)(2,1)} %all-to-all-done.exchanged), custom_call_target="tpu_custom_call" | custom-call | flops 419430400 | bytes 819200 | tf_op jit(solution)/shard_map/pallas_call | solution.py:282
  57.3 39.0 %all_to_all.15.terms = bf16[64,56,128]{2,1,0:T(8,128)(2,1)S(1)} all-to-all(bf16[64,56,128]{2,1,0:T(8,128)(2,1)S(1)} %shard_map.89), channel_id=1, replica_groups={{0,4,8,12,48,52,56,60,96,100,104,108,144,148,152,156,192,196,200,204,24..., dimensions={0} | all-to-all | bytes 1835008 | tf_op jit(solution)/shard_map/all_to_all | solution.py:309
  96.3 0.2 shard_map.90
  96.4 0.7 copy-done.1
  97.2 11.8 %all-to-all-start.2 = ((bf16[24,56,128]{2,1,0:T(8,128)(2,1)}), bf16[24,56,128]{2,1,0:T(8,128)(2,1)}, u32[]{:S(2)}, u32[]{:S(2)}) async-start(bf16[24,56,128]{2,1,0:T(8,128)(2,1)} %copy-done.1), calls=%async_computation.2 | async-start | bytes 688128 | tf_op jit(solution)/shard_map/all_to_all | solution.py:317
  109.0 2.2 %collective-permute-start.6 = (bf16[128,640]{1,0:T(8,128)(2,1)S(1)}, bf16[128,640]{1,0:T(8,128)(2,1)S(1)}, u32[]{:S(2)}, u32[]{:S(2)}) collective-permute-start(bf16[128,640]{1,0:T(8,128)(2,1)S(1)} %get-tuple-element.14), channel_id=1, source_target_pairs={{0,2},{1,3},{2,0},{3,1},{4,6},{5,7},{6,4},{7,5},{8,10},{9,11},{10,... | collective-permute-start | bytes 491528 | tf_op jit(solution)/shard_map/ppermute | solution.py:30
  111.2 5.5 %collective-permute-done.6.received = bf16[128,640]{1,0:T(8,128)(2,1)S(1)} collective-permute-done((bf16[128,640]{1,0:T(8,128)(2,1)S(1)}, bf16[128,640]{1,0:T(8,128)(2,1)S(1)}, u32[]{:S(2)}, u32[]{:S(2)}) %collective-permute-start.6) | collective-permute-done | bytes 163872 | tf_op jit(solution)/shard_map/ppermute | solution.py:30
  116.7 1.0 copy-done.2
  117.6 2.9 %shard_map.88 = bf16[128,1280]{1,0:T(8,128)(2,1)} custom-call(s32[1]{0:T(128)} %bitcast.place, bf16[256,640]{1,0:T(8,128)(2,1)} %get-tuple-element.13.attended.att, bf16[128,640]{1,0:T(8,128)(2,1)S(1)} %collective-permute-done.6.received, bf16[1280,1280]{1,0:T(8,128)(2,1)S(1)} %copy-done, bf16[128,1280]{1,0:T(8,128)(2,1)S(1)} %bitcast.7), custom_call_target="tpu_custom_call" | custom-call | flops 419430400 | bytes 3276800 | tf_op jit(solution)/shard_map/pallas_call | solution.py:289
  120.5 5.4 %all-to-all-done.2.terms = bf16[24,56,128]{2,1,0:T(8,128)(2,1)} async-done(((bf16[24,56,128]{2,1,0:T(8,128)(2,1)}), bf16[24,56,128]{2,1,0:T(8,128)(2,1)}, u32[]{:S(2)}, u32[]{:S(2)}) %all-to-all-start.2) | async-done | bytes 344096 | tf_op jit(solution)/shard_map/all_to_all | solution.py:317
  125.9 1.7 %shard_map.91 = f32[40,1280]{1,0:T(8,128)} custom-call(bf16[24,56,128]{2,1,0:T(8,128)(2,1)} %all-to-all-done.2.terms), custom_call_target="tpu_custom_call" | custom-call | flops 172032 | bytes 344064 | tf_op jit(solution)/shard_map/pallas_call | solution.py:318
  (7 shorter events, 0.0 us)
Async XLA Ops:
  3.8 21.4 %collective-permute-start.1 = (bf16[2,128,640]{2,1,0:T(8,128)(2,1)}, bf16[2,128,640]{2,1,0:T(8,128)(2,1)S(1)}, u32[]{:S(2)}, u32[]{:S(2)}) collective-permute-start(bf16[2,128,640]{2,1,0:T(8,128)(2,1)} %get-tuple-element.12), channel_id=1, source_target_pairs={{0,2},{1,3},{2,0},{3,1},{4,6},{5,7},{6,4},{7,5},{8,10},{9,11},{10,... | collective-permute-start | bytes 983048 | tf_op jit(solution)/shard_map/ppermute | solution.py:30
  15.2 38.2 %all-to-all-start = ((bf16[4,128,640]{2,1,0:T(8,128)(2,1)}), bf16[4,128,640]{2,1,0:T(8,128)(2,1)}, u32[]{:S(2)}, u32[]{:S(2)}) async-start(bf16[4,128,640]{2,1,0:T(8,128)(2,1)} %get-tuple-element.15), calls=%async_computation | async-start | bytes 1310720 | tf_op jit(solution)/shard_map/all_to_all | solution.py:258
  19.3 19.2 %collective-permute-start.4 = (bf16[2,128,640]{2,1,0:T(8,128)(2,1)}, bf16[2,128,640]{2,1,0:T(8,128)(2,1)S(1)}, u32[]{:S(2)}, u32[]{:S(2)}) collective-permute-start(bf16[2,128,640]{2,1,0:T(8,128)(2,1)} %get-tuple-element.11.kv_own), channel_id=1, source_target_pairs={{4,0},{5,1},{6,2},{7,3},{8,4},{9,5},{10,6},{11,7},{12,8},{13,9},{1... | collective-permute-start | bytes 983048 | tf_op jit(solution)/shard_map/ppermute | solution.py:30
  20.6 17.9 %collective-permute-start.2 = (bf16[2,128,640]{2,1,0:T(8,128)(2,1)}, bf16[2,128,640]{2,1,0:T(8,128)(2,1)S(1)}, u32[]{:S(2)}, u32[]{:S(2)}) collective-permute-start(bf16[2,128,640]{2,1,0:T(8,128)(2,1)} %get-tuple-element.11.kv_own), channel_id=1, source_target_pairs={{0,4},{1,5},{2,6},{3,7},{4,8},{5,9},{6,10},{7,11},{8,12},{9,13},{1... | collective-permute-start | bytes 983048 | tf_op jit(solution)/shard_map/ppermute | solution.py:30
  25.2 13.3 %collective-permute-start.5 = (bf16[2,128,640]{2,1,0:T(8,128)(2,1)S(1)}, bf16[2,128,640]{2,1,0:T(8,128)(2,1)S(1)}, u32[]{:S(2)}, u32[]{:S(2)}) collective-permute-start(bf16[2,128,640]{2,1,0:T(8,128)(2,1)S(1)} %collective-permute-done.1.kv_pair), channel_id=1, source_target_pairs={{4,0},{5,1},{6,2},{7,3},{8,4},{9,5},{10,6},{11,7},{12,8},{13,9},{1... | collective-permute-start | bytes 983048 | tf_op jit(solution)/shard_map/ppermute | solution.py:30
  26.5 12.8 %collective-permute-start.3 = (bf16[2,128,640]{2,1,0:T(8,128)(2,1)S(1)}, bf16[2,128,640]{2,1,0:T(8,128)(2,1)S(1)}, u32[]{:S(2)}, u32[]{:S(2)}) collective-permute-start(bf16[2,128,640]{2,1,0:T(8,128)(2,1)S(1)} %collective-permute-done.1.kv_pair), channel_id=1, source_target_pairs={{0,4},{1,5},{2,6},{3,7},{4,8},{5,9},{6,10},{7,11},{8,12},{9,13},{1... | collective-permute-start | bytes 983048 | tf_op jit(solution)/shard_map/ppermute | solution.py:30
  31.1 7.4 %collective-permute-start = (bf16[128,640]{1,0:T(8,128)(2,1)}, bf16[128,640]{1,0:T(8,128)(2,1)S(1)}, u32[]{:S(2)}, u32[]{:S(2)}) collective-permute-start(bf16[128,640]{1,0:T(8,128)(2,1)} %get-tuple-element.10), channel_id=1, source_target_pairs={{0,2},{1,3},{2,0},{3,1},{4,6},{5,7},{6,4},{7,5},{8,10},{9,11},{10,... | collective-permute-start | bytes 491528 | tf_op jit(solution)/shard_map/ppermute | solution.py:30
  39.3 1.0 copy-start.3
  40.3 0.9 copy-start.4
  41.2 0.7 copy-start.5
  51.1 65.5 %copy-start = (bf16[1280,1280]{1,0:T(8,128)(2,1)S(1)}, bf16[1280,1280]{1,0:T(8,128)(2,1)}, u32[]{:S(2)}) copy-start(bf16[1280,1280]{1,0:T(8,128)(2,1)} %weight.1) | copy-start | bytes 9830404
  51.1 4.1 %collective-permute-start.7 = (bf16[256,640]{1,0:T(8,128)(2,1)}, bf16[256,640]{1,0:T(8,128)(2,1)}, u32[]{:S(2)}, u32[]{:S(2)}) collective-permute-start(bf16[256,640]{1,0:T(8,128)(2,1)} %get-tuple-element.13.attended.att), channel_id=1, source_target_pairs={{0,1},{1,0},{2,3},{3,2},{4,5},{5,4},{6,7},{7,6},{8,9},{9,8},{10,11... | collective-permute-start | bytes 983048 | tf_op jit(solution)/shard_map/ppermute | solution.py:30
  96.4 0.7 copy-start.1
  97.2 28.8 %all-to-all-start.2 = ((bf16[24,56,128]{2,1,0:T(8,128)(2,1)}), bf16[24,56,128]{2,1,0:T(8,128)(2,1)}, u32[]{:S(2)}, u32[]{:S(2)}) async-start(bf16[24,56,128]{2,1,0:T(8,128)(2,1)} %copy-done.1), calls=%async_computation.2 | async-start | bytes 688128 | tf_op jit(solution)/shard_map/all_to_all | solution.py:317
  109.0 7.7 %collective-permute-start.6 = (bf16[128,640]{1,0:T(8,128)(2,1)S(1)}, bf16[128,640]{1,0:T(8,128)(2,1)S(1)}, u32[]{:S(2)}, u32[]{:S(2)}) collective-permute-start(bf16[128,640]{1,0:T(8,128)(2,1)S(1)} %get-tuple-element.14), channel_id=1, source_target_pairs={{0,2},{1,3},{2,0},{3,1},{4,6},{5,7},{6,4},{7,5},{8,10},{9,11},{10,... | collective-permute-start | bytes 491528 | tf_op jit(solution)/shard_map/ppermute | solution.py:30
  116.7 1.0 copy-start.2

commit v2 on v1

v2 whole, which is shorter than its diff:
```python
import functools

import jax
import jax.numpy as jnp
from jax import lax
from jax.experimental import pallas as pl
from jax.experimental.pallas import tpu as pltpu
from jax.sharding import PartitionSpec as P


HEADS = 16
LOG2E = 1.4426950408889634
AXES = ("section", "seq", "dp")
ANY = pl.BlockSpec(memory_space=pl.ANY)
HBM = pl.BlockSpec(memory_space=pltpu.HBM)
VMEM = pl.BlockSpec(memory_space=pltpu.VMEM)
SMEM = pl.BlockSpec(memory_space=pltpu.SMEM)
NT = (((1,), (1,)), ((), ()))
TT = (((0,), (1,)), ((), ()))


def moved(value, target):
    sections, seqs, cores = (lax.axis_size(axis) for axis in AXES)
    pairs = []
    for section in range(sections):
        for seq in range(seqs):
            for core in range(cores):
                to_seq, to_core = target(seq, core)
                if 0 <= to_seq < seqs:
                    source = (section * seqs + seq) * cores + core
                    pairs.append((source, (section * seqs + to_seq) * cores + to_core))
    return lax.ppermute(value, AXES, pairs)


def to_pair(value):
    return moved(value, lambda seq, core: (seq ^ 1, core))


def to_core(value):
    return moved(value, lambda seq, core: (seq, 1 - core))


def to_next(value):
    return moved(value, lambda seq, core: (seq + 2, core))


def to_previous(value):
    return moved(value, lambda seq, core: (seq - 2, core))


def position(place):
    index = place[0]
    return index >> 2, (index >> 1) & 1, index & 1


def split_kernel(
    width, place, query, key, value, cotangent, kv_own, kv_other, q_own, q_other, exchanged
):
    _, y, _ = position(place)
    half = q_own.shape[1]
    own = pl.ds(pl.multiple_of(y * half, half), half)
    other = pl.ds(pl.multiple_of((1 - y) * half, half), half)
    for part, out in ((own, kv_own), (other, kv_other)):
        out[0] = key[:, part]
        chosen = value[:, part]
        for first in range(0, half, 128):
            out[1, :, first : first + 128] = jnp.transpose(chosen[:, first : first + 128])
    q_own[...] = query[:, own]
    q_other[...] = query[:, other]
    picked = half // 2
    shift = 20
    factor = -(-(1 << shift) // width)
    assert all((j * factor) >> shift == j // width for j in range(picked))
    row = lax.broadcasted_iota(jnp.int32, (picked, half), 0)
    column = lax.broadcasted_iota(jnp.int32, (picked, half), 1)
    base = row + lax.shift_right_logical(row * factor, shift) * width
    for to_core_index in range(2):
        chosen = (column == base + to_core_index * width).astype(jnp.float32)
        chosen = chosen.astype(jnp.bfloat16)
        for part in range(2):
            block = lax.dot_general(
                chosen,
                cotangent[:, part * half : (part + 1) * half],
                NT,
                preferred_element_type=jnp.float32,
            ).astype(jnp.bfloat16)
            for side in range(2):
                exchanged[
                    side * 2 + to_core_index, part * picked : (part + 1) * picked, :
                ] = block


def attention_kernel(
    head_dim, place, segments, q_own, q_pair, kv_own, kv_pair, kv_left, kv_left_pair,
    kv_right, kv_right_pair, attended, passed, queries, keys, values, bias, scores, probs, sems
):
    rows, half = q_own.shape
    total = segments.shape[1]
    heads = half // head_dim
    z, y, _ = position(place)
    blocks = (kv_own, kv_pair, kv_left, kv_left_pair, kv_right, kv_right_pair)
    moves = [(q_own, queries.at[pl.ds(0, rows)]), (q_pair, queries.at[pl.ds(rows, rows)])]
    for i, block in enumerate(blocks):
        here = pl.ds(i * rows, rows)
        moves.append((block.at[0], keys.at[here]))
        for first in range(0, half, 128):
            some = pl.ds(first, 128)
            moves.append((block.at[1, :, some], values.at[some, here]))
    copies = [
        pltpu.make_async_copy(source, target, sems.at[i])
        for i, (source, target) in enumerate(moves)
    ]
    for copy in copies:
        copy.start()
    ids = []
    for i in range(6):
        offset = ((z + (0, -1, 1)[i // 2]) * 2 + (y if i % 2 == 0 else 1 - y)) * rows
        start = pl.multiple_of(jnp.clip(offset, 0, total - rows), rows)
        row = segments[:, pl.ds(start, rows)]
        ids.append(jnp.where((offset >= 0) & (offset < total), row, -1))
    for i in range(6):
        key_ids = jnp.transpose(jnp.broadcast_to(ids[i], (rows, rows)))
        for j in range(2):
            bias[i * rows : (i + 1) * rows, j * rows : (j + 1) * rows] = jnp.where(
                key_ids == ids[j], jnp.float32(0.0), jnp.float32(-1e30)
            )
    for copy in copies:
        copy.wait()
    scale = head_dim ** (-0.5) * LOG2E
    ones = jnp.ones((16, 6 * rows), jnp.bfloat16)
    step = 64

    def multiply(head):
        first, last = head * head_dim, (head + 1) * head_dim
        low, high = first // 128 * 128, -(-last // 128) * 128
        lane = lax.broadcasted_iota(jnp.int32, (2 * rows, high - low), 1) + low
        inside = (lane >= first) & (lane < last)
        query = jnp.where(inside, queries[:, low:high], jnp.zeros((), jnp.bfloat16))
        found = lax.dot_general(
            keys[:, low:high], query, NT, preferred_element_type=jnp.float32
        )
        found = found + bias[...]
        scores[head % 2] = found
        return jnp.max(found, axis=0, keepdims=True)

    highest = multiply(0)
    for head in range(heads):
        following = multiply(head + 1) if head + 1 < heads else None
        for low in range(0, 6 * rows, step):
            some = slice(low, low + step)
            expo = jnp.exp2((scores[head % 2, some, :] - highest) * scale)
            probs[head % 2, some, :] = expo.astype(jnp.bfloat16)
        here = slice(head * head_dim, (head + 1) * head_dim)
        weighted = jnp.dot(
            jnp.concatenate([values[here, :], ones], axis=0),
            probs[head % 2],
            preferred_element_type=jnp.float32,
        )
        norm = 1.0 / weighted[head_dim : head_dim + 1, :]
        result = (weighted[:head_dim, :] * norm).astype(jnp.bfloat16)
        attended[here, :] = result
        passed[here, :] = result[:, rows:]
        highest = following


def gradient_kernel(place, att, att_core, exchanged, out):
    _, y, core = position(place)
    order = (2 * y + core, 2 * (1 - y) + core, 2 * y + 1 - core, 2 * (1 - y) + 1 - core)
    left = jnp.concatenate([exchanged[index] for index in order], axis=1)
    right = jnp.concatenate([att[...], att_core[...]], axis=1)
    out[...] = lax.dot_general(left, right, NT, preferred_element_type=jnp.float32).astype(
        jnp.bfloat16
    )


def first_sum_kernel(width, terms, out):
    parts = out.shape[0] // (terms.shape[1] // width)
    tall = out.shape[1]
    for block in range(terms.shape[1] // width):
        some = slice(block * width, (block + 1) * width)
        total = sum(terms[i, some, :].astype(jnp.float32) for i in range(terms.shape[0]))
        for part in range(parts):
            column, row = part // 2 * 128, part % 2 * tall
            if column < terms.shape[2]:
                tile = total[row : row + tall, column : column + 128]
                if tile.shape[0] < tall:
                    tile = jnp.concatenate(
                        [tile, jnp.zeros((tall - tile.shape[0], 128), jnp.float32)], axis=0
                    )
            else:
                tile = jnp.zeros((tall, 128), jnp.float32)
            out[block * parts + part] = tile.astype(jnp.bfloat16)


def second_sum_kernel(scale, terms, out):
    total = sum(terms[i].astype(jnp.float32) for i in range(terms.shape[0])) * scale
    total = total.astype(jnp.bfloat16)
    for i in range(out.shape[0]):
        out[i] = total


def assembly_kernel(terms, out):
    width, features = out.shape
    tall = terms.shape[1]
    for side in range(2):
        for part in range(features // 128):
            row = part % 2 * tall
            rows = min(tall, width - row)
            column = side * (features // 2) + part // 2 * 128
            tile = terms[part * 2 + side].astype(jnp.float32)
            out[row : row + rows, column : column + 128] = tile[:rows, :]


def projection_kernel(place, attended, received, weight, residual, out):
    half, rows = received.shape
    _, y, _ = position(place)
    own = pl.ds(pl.multiple_of(y * half, half), half)
    other = pl.ds(pl.multiple_of((1 - y) * half, half), half)
    total = lax.dot_general(
        attended[:, :rows], weight[:, own], TT, preferred_element_type=jnp.float32
    )
    total += lax.dot_general(
        received[...], weight[:, other], TT, preferred_element_type=jnp.float32
    )
    out[...] = (residual[...].astype(jnp.float32) + total).astype(jnp.bfloat16)


def call(kernel, outs, in_specs, flops, moved_bytes, scratch=(), grant=16):
    return pl.pallas_call(
        kernel,
        out_shape=outs,
        in_specs=in_specs,
        out_specs=jax.tree.map(lambda _: VMEM, outs),
        scratch_shapes=scratch,
        cost_estimate=pl.CostEstimate(
            flops=flops, bytes_accessed=moved_bytes, transcendentals=0
        ),
        compiler_params=pltpu.CompilerParams(vmem_limit_bytes=grant << 20),
    )


def per_device(queries, key_input, value_input, residual, segments, out_weight, cotangent):
    rows, features = queries.shape[1], queries.shape[2]
    half = features // 2
    head_dim = features // HEADS
    sections, seqs, cores = (lax.axis_size(axis) for axis in AXES)
    units = seqs // 2
    width = features // (sections * cores)
    place = lax.axis_index(("seq", "dp")).astype(jnp.int32).reshape(1)

    def bf16(*shape):
        return jax.ShapeDtypeStruct(shape, jnp.bfloat16)

    kv_own, kv_other, q_own, q_other, exchanged = call(
        functools.partial(split_kernel, width),
        (
            bf16(2, rows, half),
            bf16(2, rows, half),
            bf16(rows, half),
            bf16(rows, half),
            bf16(4, half, rows),
        ),
        [SMEM, VMEM, VMEM, VMEM, VMEM],
        2 * half * features * rows,
        24 * rows * features,
        grant=62,
    )(place, queries[0], key_input[0], value_input[0], cotangent[0])
    kv_pair = to_pair(kv_other)
    kv_left = to_next(kv_own)
    kv_right = to_previous(kv_own)
    kv_left_pair = to_next(kv_pair)
    kv_right_pair = to_previous(kv_pair)
    q_pair = to_pair(q_other)
    quads = [list(range(first, first + 4)) for first in range(0, 2 * seqs, 4)]
    exchanged = lax.all_to_all(exchanged, ("seq", "dp"), 0, 0, tiled=True, axis_index_groups=quads)
    attended, passed = call(
        functools.partial(attention_kernel, head_dim),
        (bf16(half, 2 * rows), bf16(half, rows)),
        [SMEM, VMEM] + [ANY] * 8,
        4 * 2 * rows * 6 * rows * half,
        26 * rows * half,
        scratch=[
            pltpu.VMEM((2 * rows, half), jnp.bfloat16),
            pltpu.VMEM((6 * rows, half), jnp.bfloat16),
            pltpu.VMEM((half, 6 * rows), jnp.bfloat16),
            pltpu.VMEM((6 * rows, 2 * rows), jnp.float32),
            pltpu.VMEM((2, 6 * rows, 2 * rows), jnp.float32),
            pltpu.VMEM((2, 6 * rows, 2 * rows), jnp.bfloat16),
            pltpu.SemaphoreType.DMA((2 + 6 * (1 + half // 128),)),
        ],
        grant=16,
    )(
        place, segments, q_own, q_pair, kv_own, kv_pair, kv_left, kv_left_pair,
        kv_right, kv_right_pair,
    )
    attended_core = to_core(attended)
    received = to_pair(passed)
    partial = call(
        gradient_kernel,
        bf16(half, half),
        [SMEM, VMEM, VMEM, VMEM],
        2 * half * half * 4 * rows,
        2 * half * half,
        grant=62,
    )(place, attended, attended_core, exchanged)
    mixed_out = call(
        projection_kernel,
        bf16(rows, features),
        [SMEM] + [VMEM] * 4,
        2 * rows * features * features,
        2 * features * features,
        grant=16,
    )(place, attended, received, out_weight, residual[0])

    groups = sections * cores
    grad_scale = 1.0 / float(groups * seqs * rows) ** 0.5
    side_x, side_y = 4, sections // 4
    parts, tall = units, 24
    lines = [
        [(x * side_y + y) for x in range(side_x)] for y in range(side_y)
    ]
    terms = lax.all_to_all(
        partial.reshape(side_x, side_y * width, half),
        "section",
        0,
        0,
        tiled=True,
        axis_index_groups=lines,
    )
    terms = call(
        functools.partial(first_sum_kernel, width),
        bf16(side_y * parts, tall, 128),
        [VMEM],
        half * half,
        3 * half * half,
    )(terms)
    planes = [
        [
            ((x * side_y + y) * seqs + (first + part) * 2 + side) * cores + core
            for y in range(side_y)
            for part in range(parts)
        ]
        for x in range(side_x)
        for first in range(0, units, parts)
        for side in range(2)
        for core in range(cores)
    ]
    terms = lax.all_to_all(terms, AXES, 0, 0, tiled=True, axis_index_groups=planes)
    spread = call(
        functools.partial(second_sum_kernel, grad_scale),
        bf16(seqs, tall, 128),
        [VMEM],
        side_y * parts * tall * 128,
        2 * (side_y * parts + seqs) * tall * 128,
    )(terms)
    spread = lax.all_to_all(spread, "seq", 0, 0, tiled=True)
    weight_grad = call(
        assembly_kernel,
        jax.ShapeDtypeStruct((width, features), jnp.float32),
        [VMEM],
        seqs * tall * 128,
        2 * seqs * tall * 128,
    )(spread)
    return (mixed_out[None], weight_grad)


def solution(mesh):
    in_specs = (
        P(("section", "dp"), "seq", None),
        P(("section", "dp"), "seq", None),
        P(("section", "dp"), "seq", None),
        P(("section", "dp"), "seq", None),
        P(("section", "dp"), None),
        P(),
        P(("section", "dp"), "seq", None),
    )
    out_specs = (P(("section", "dp"), "seq", None), P(("section", "dp"), None))
    return jax.shard_map(
        per_device, mesh=mesh, in_specs=in_specs, out_specs=out_specs, check_vma=False
    )
```

time: 128 us -> 125 us (0.977)
  blocking collectives: 39 us -> 52.5 us
  starting transfers between devices: 45.3 us -> 37.2 us
  waiting for transfers between devices: 19.2 us -> 13.6 us
  Pallas kernels: 19.1 us -> 14.6 us
  local copies, waits for them, and re-layouts: 4.3 us -> 5.93 us
    all_to_all x1 -> x2, blocking collectives: 39 us -> 52.5 us  [the longest x1 35.5 us: per_device(): lax.all_to_all(terms, AXES, 0, 0, tiled=True, axis_index_groups=planes)]
    all_to_all x1, starting transfers between devices: 11.8 us -> 4.78 us  [per_device(): spread = lax.all_to_all(spread, 'seq', 0, 0, tiled=True)]
    all_to_all x1, waiting for transfers between devices: 5.43 us -> 0.01 us  [per_device(): spread = lax.all_to_all(spread, 'seq', 0, 0, tiled=True)]
    pallas_call x4 -> x5, Pallas kernels: 13.1 us -> 9.62 us  [the longest x1 5.22 us: per_device(): call(functools.partial(attention_kernel, head_dim), (bf16(half, 2 * rows)...]
    unnamed x12 -> x20, local copies, waits for them, and re-layouts: 4.3 us -> 5.93 us
  transfers between devices with their start and end apart: 10 -> 10, of which waited for: 5 -> 4; matrix products, arithmetic and copies ran while one was open for 0% -> 0% of each run, Pallas kernels for 9% -> 6%
where the time goes in v2:
time: 125 us
  blocking collectives  52.5 us (42%)
  starting transfers between devices  37.2 us (30%)
  Pallas kernels  14.6 us (12%)
  waiting for transfers between devices  13.6 us (11%)
  local copies, waits for them, and re-layouts  5.93 us (5%)
    all_to_all x1, blocking collectives, per_device(): lax.all_to_all(terms, AXES, 0, 0, tiled=True, axis_index_groups=planes)  35.5 us
    ppermute x8, starting transfers between devices, moved(): return lax.ppermute(value, AXES, pairs)  29 us
    all_to_all x1, blocking collectives, per_device(): lax.all_to_all(partial.reshape(side_x, side_y * width, half), 'section',...  16.9 us
    ppermute x8, waiting for transfers between devices, moved(): return lax.ppermute(value, AXES, pairs)  13.6 us
    unnamed x20, local copies, waits for them, and re-layouts  5.93 us
    pallas_call x1, Pallas kernels, per_device(): call(functools.partial(attention_kernel, head_dim), (bf16(half, 2 * rows)...  5.22 us
    all_to_all x1, starting transfers between devices, per_device(): spread = lax.all_to_all(spread, 'seq', 0, 0, tiled=True)  4.78 us
    all_to_all x1, starting transfers between devices, per_device(): lax.all_to_all(exchanged, ('seq', 'dp'), 0, 0, tiled=True, axis_index_gro...  3.48 us
  transfers between devices with their start and end apart: 10, of which 4 were waited for; matrix products, arithmetic and copies ran while one was open for 0% of the time, Pallas kernels for 6%

profile of v2, /device:TPU:8, one launch (start us, length us, event | category | flops | bytes accessed | tf_op | source)
XLA Modules:
  0.0 124.6 jit_solution(16238908946362070618)
XLA Ops:
  0.6 3.0 %shard_map.86 = (bf16[2,128,640]{2,1,0:T(8,128)(2,1)}, bf16[2,128,640]{2,1,0:T(8,128)(2,1)}, bf16[128,640]{1,0:T(8,128)(2,1)}, bf16[128,640]{1,0:T(8,128)(2,1)}, bf16[4,640,128]{2,1,0:T(8,128)(2,1)}) custom-call(s32[1]{0:T(128)} %bitcast.place, bf16[128,1280]{1,0:T(8,128)(2,1)} %bitcast.11, bf16[128,1280]{1,0:T(8,128)(2,1)} %bitcast.12, ...), custom_call_target="tpu_custom_call" | custom-call | flops 209715200 | bytes 3932160 | tf_op jit(solution)/shard_map/pallas_call | solution.py:254
  3.7 11.3 %collective-permute-start.1 = (bf16[2,128,640]{2,1,0:T(8,128)(2,1)}, bf16[2,128,640]{2,1,0:T(8,128)(2,1)S(1)}, u32[]{:S(2)}, u32[]{:S(2)}) collective-permute-start(bf16[2,128,640]{2,1,0:T(8,128)(2,1)} %get-tuple-element.12), channel_id=1, source_target_pairs={{0,2},{1,3},{2,0},{3,1},{4,6},{5,7},{6,4},{7,5},{8,10},{9,11},{10,... | collective-permute-start | bytes 983048 | tf_op jit(solution)/shard_map/ppermute | solution.py:32
  15.0 3.5 %all-to-all-start = ((bf16[4,640,128]{2,1,0:T(8,128)(2,1)}), bf16[4,640,128]{2,1,0:T(8,128)(2,1)S(1)}, u32[]{:S(2)}, u32[]{:S(2)}) async-start(bf16[4,640,128]{2,1,0:T(8,128)(2,1)} %get-tuple-element.15), calls=%async_computation | async-start | bytes 1310720 | tf_op jit(solution)/shard_map/all_to_all | solution.py:275
  18.5 1.3 %collective-permute-start.4 = (bf16[2,128,640]{2,1,0:T(8,128)(2,1)}, bf16[2,128,640]{2,1,0:T(8,128)(2,1)S(1)}, u32[]{:S(2)}, u32[]{:S(2)}) collective-permute-start(bf16[2,128,640]{2,1,0:T(8,128)(2,1)} %get-tuple-element.11.kv_own), channel_id=1, source_target_pairs={{4,0},{5,1},{6,2},{7,3},{8,4},{9,5},{10,6},{11,7},{12,8},{13,9},{1... | collective-permute-start | bytes 983048 | tf_op jit(solution)/shard_map/ppermute | solution.py:32
  19.8 4.6 %collective-permute-start.2 = (bf16[2,128,640]{2,1,0:T(8,128)(2,1)}, bf16[2,128,640]{2,1,0:T(8,128)(2,1)S(1)}, u32[]{:S(2)}, u32[]{:S(2)}) collective-permute-start(bf16[2,128,640]{2,1,0:T(8,128)(2,1)} %get-tuple-element.11.kv_own), channel_id=1, source_target_pairs={{0,4},{1,5},{2,6},{3,7},{4,8},{5,9},{6,10},{7,11},{8,12},{9,13},{1... | collective-permute-start | bytes 983048 | tf_op jit(solution)/shard_map/ppermute | solution.py:32
  24.4 0.0 collective-permute-done.1.kv_pair
  24.4 1.3 %collective-permute-start.5 = (bf16[2,128,640]{2,1,0:T(8,128)(2,1)S(1)}, bf16[2,128,640]{2,1,0:T(8,128)(2,1)S(1)}, u32[]{:S(2)}, u32[]{:S(2)}) collective-permute-start(bf16[2,128,640]{2,1,0:T(8,128)(2,1)S(1)} %collective-permute-done.1.kv_pair), channel_id=1, source_target_pairs={{4,0},{5,1},{6,2},{7,3},{8,4},{9,5},{10,6},{11,7},{12,8},{13,9},{1... | collective-permute-start | bytes 983048 | tf_op jit(solution)/shard_map/ppermute | solution.py:32
  25.7 4.6 %collective-permute-start.3 = (bf16[2,128,640]{2,1,0:T(8,128)(2,1)S(1)}, bf16[2,128,640]{2,1,0:T(8,128)(2,1)S(1)}, u32[]{:S(2)}, u32[]{:S(2)}) collective-permute-start(bf16[2,128,640]{2,1,0:T(8,128)(2,1)S(1)} %collective-permute-done.1.kv_pair), channel_id=1, source_target_pairs={{0,4},{1,5},{2,6},{3,7},{4,8},{5,9},{6,10},{7,11},{8,12},{9,13},{1... | collective-permute-start | bytes 983048 | tf_op jit(solution)/shard_map/ppermute | solution.py:32
  30.3 1.9 %collective-permute-start = (bf16[128,640]{1,0:T(8,128)(2,1)}, bf16[128,640]{1,0:T(8,128)(2,1)S(1)}, u32[]{:S(2)}, u32[]{:S(2)}) collective-permute-start(bf16[128,640]{1,0:T(8,128)(2,1)} %get-tuple-element.10), channel_id=1, source_target_pairs={{0,2},{1,3},{2,0},{3,1},{4,6},{5,7},{6,4},{7,5},{8,10},{9,11},{10,... | collective-permute-start | bytes 491528 | tf_op jit(solution)/shard_map/ppermute | solution.py:32
  32.2 5.5 %collective-permute-done.q_pair = bf16[128,640]{1,0:T(8,128)(2,1)S(1)} collective-permute-done((bf16[128,640]{1,0:T(8,128)(2,1)}, bf16[128,640]{1,0:T(8,128)(2,1)S(1)}, u32[]{:S(2)}, u32[]{:S(2)}) %collective-permute-start) | collective-permute-done | bytes 163872 | tf_op jit(solution)/shard_map/ppermute | solution.py:32
  37.7 0.8 collective-permute-done.3.kv_left_pair
  38.5 1.0 copy-done.4
  39.5 0.9 copy-done.5
  40.4 0.7 copy-done.6
  41.1 5.2 %shard_map.87 = (bf16[640,256]{1,0:T(8,128)(2,1)S(1)}, bf16[640,128]{1,0:T(8,128)(2,1)S(1)}) custom-call(s32[1]{0:T(128)} %bitcast.place, s32[1,3072]{1,0:T(1,128)S(1)} %copy-done.6, bf16[128,640]{1,0:T(8,128)(2,1)S(1)} %copy-done.5, bf16[128,640]{1,0:T(8,128)(2,1)S(1)} %collective-permute-done.q_pair, bf16[2,128,640]{2,1,0:T(8,128)(2,1)S(1)} %copy-done.4, ...), custom_call_target="tpu_custom_call" | custom-call | flops 503316480 | bytes 2129920 | tf_op jit(solution)/shard_map/pallas_call | solution.py:276
  46.3 0.0 copy-start.7
  46.3 0.7 copy-done.7
  47.0 1.9 %collective-permute-start.7 = (bf16[640,256]{1,0:T(8,128)(2,1)S(1)}, bf16[640,256]{1,0:T(8,128)(2,1)S(1)}, u32[]{:S(2)}, u32[]{:S(2)}) collective-permute-start(bf16[640,256]{1,0:T(8,128)(2,1)S(1)} %get-tuple-element.13.attended.att), channel_id=1, source_target_pairs={{0,1},{1,0},{2,3},{3,2},{4,5},{5,4},{6,7},{7,6},{8,9},{9,8},{10,11... | collective-permute-start | bytes 983048 | tf_op jit(solution)/shard_map/ppermute | solution.py:32
  48.9 1.6 %collective-permute-done.7.att_core = bf16[640,256]{1,0:T(8,128)(2,1)S(1)} collective-permute-done((bf16[640,256]{1,0:T(8,128)(2,1)S(1)}, bf16[640,256]{1,0:T(8,128)(2,1)S(1)}, u32[]{:S(2)}, u32[]{:S(2)}) %collective-permute-start.7) | collective-permute-done | bytes 327712 | tf_op jit(solution)/shard_map/ppermute | solution.py:32
  50.5 0.7 copy-done.9
  51.2 2.9 %shard_map.89 = bf16[640,640]{1,0:T(8,128)(2,1)} custom-call(s32[1]{0:T(128)} %bitcast.place, bf16[640,256]{1,0:T(8,128)(2,1)} %copy-done.1, bf16[640,256]{1,0:T(8,128)(2,1)} %copy-done.9, bf16[4,640,128]{2,1,0:T(8,128)(2,1)} %copy-done.8), custom_call_target="tpu_custom_call" | custom-call | flops 419430400 | bytes 819200 | tf_op jit(solution)/shard_map/pallas_call | solution.py:298
  54.1 16.9 %all_to_all.20.terms = bf16[4,160,640]{2,1,0:T(8,128)(2,1)S(1)} all-to-all(bf16[4,160,640]{2,1,0:T(8,128)(2,1)} %bitcast.9), channel_id=1, replica_groups={{0,192,384,576},{48,240,432,624},{96,288,480,672},{144,336,528,720},{1,..., dimensions={0} | all-to-all | bytes 1638400 | tf_op jit(solution)/shard_map/all_to_all | solution.py:322
  71.1 0.1 shard_map.90
  71.2 35.5 %all_to_all.21.terms = bf16[48,24,128]{2,1,0:T(8,128)(2,1)S(1)} all-to-all(bf16[48,24,128]{2,1,0:T(8,128)(2,1)S(1)} %shard_map.90), channel_id=1, replica_groups={{0,4,8,12,16,20,24,28,32,36,40,44,48,52,56,60,64,68,72,76,80,84,88,92,9..., dimensions={0} | all-to-all | bytes 589824 | tf_op jit(solution)/shard_map/all_to_all | solution.py:348
  106.7 0.7 shard_map.91
  107.4 4.8 %all-to-all-start.3 = ((bf16[24,24,128]{2,1,0:T(8,128)(2,1)}), bf16[24,24,128]{2,1,0:T(8,128)(2,1)S(1)}, u32[]{:S(2)}, u32[]{:S(2)}) async-start(bf16[24,24,128]{2,1,0:T(8,128)(2,1)} %shard_map.91), calls=%async_computation.3 | async-start | bytes 294912 | tf_op jit(solution)/shard_map/all_to_all | solution.py:356
  112.2 2.1 %collective-permute-start.6 = (bf16[640,128]{1,0:T(8,128)(2,1)}, bf16[640,128]{1,0:T(8,128)(2,1)S(1)}, u32[]{:S(2)}, u32[]{:S(2)}) collective-permute-start(bf16[640,128]{1,0:T(8,128)(2,1)} %copy-done.7), channel_id=1, source_target_pairs={{0,2},{1,3},{2,0},{3,1},{4,6},{5,7},{6,4},{7,5},{8,10},{9,11},{10,... | collective-permute-start | bytes 491528 | tf_op jit(solution)/shard_map/ppermute | solution.py:32
  114.3 5.7 %collective-permute-done.6.received = bf16[640,128]{1,0:T(8,128)(2,1)S(1)} collective-permute-done((bf16[640,128]{1,0:T(8,128)(2,1)}, bf16[640,128]{1,0:T(8,128)(2,1)S(1)}, u32[]{:S(2)}, u32[]{:S(2)}) %collective-permute-start.6) | collective-permute-done | bytes 163872 | tf_op jit(solution)/shard_map/ppermute | solution.py:32
  120.0 1.0 copy-done.2
  121.0 1.0 copy-done.3
  122.0 1.9 %shard_map.88 = bf16[128,1280]{1,0:T(8,128)(2,1)} custom-call(s32[1]{0:T(128)} %bitcast.place, bf16[640,256]{1,0:T(8,128)(2,1)S(1)} %copy-done.2, bf16[640,128]{1,0:T(8,128)(2,1)S(1)} %collective-permute-done.6.received, bf16[1280,1280]{1,0:T(8,128)(2,1)S(1)} %copy-done, bf16[128,1280]{1,0:T(8,128)(2,1)S(1)} %bitcast.8), custom_call_target="tpu_custom_call" | custom-call | flops 419430400 | bytes 3276800 | tf_op jit(solution)/shard_map/pallas_call | solution.py:306
  123.9 0.7 shard_map.92
  (17 shorter events, 0.0 us)
Async XLA Ops:
  3.7 20.7 %collective-permute-start.1 = (bf16[2,128,640]{2,1,0:T(8,128)(2,1)}, bf16[2,128,640]{2,1,0:T(8,128)(2,1)S(1)}, u32[]{:S(2)}, u32[]{:S(2)}) collective-permute-start(bf16[2,128,640]{2,1,0:T(8,128)(2,1)} %get-tuple-element.12), channel_id=1, source_target_pairs={{0,2},{1,3},{2,0},{3,1},{4,6},{5,7},{6,4},{7,5},{8,10},{9,11},{10,... | collective-permute-start | bytes 983048 | tf_op jit(solution)/shard_map/ppermute | solution.py:32
  15.0 33.9 %all-to-all-start = ((bf16[4,640,128]{2,1,0:T(8,128)(2,1)}), bf16[4,640,128]{2,1,0:T(8,128)(2,1)S(1)}, u32[]{:S(2)}, u32[]{:S(2)}) async-start(bf16[4,640,128]{2,1,0:T(8,128)(2,1)} %get-tuple-element.15), calls=%async_computation | async-start | bytes 1310720 | tf_op jit(solution)/shard_map/all_to_all | solution.py:275
  18.5 19.2 %collective-permute-start.4 = (bf16[2,128,640]{2,1,0:T(8,128)(2,1)}, bf16[2,128,640]{2,1,0:T(8,128)(2,1)S(1)}, u32[]{:S(2)}, u32[]{:S(2)}) collective-permute-start(bf16[2,128,640]{2,1,0:T(8,128)(2,1)} %get-tuple-element.11.kv_own), channel_id=1, source_target_pairs={{4,0},{5,1},{6,2},{7,3},{8,4},{9,5},{10,6},{11,7},{12,8},{13,9},{1... | collective-permute-start | bytes 983048 | tf_op jit(solution)/shard_map/ppermute | solution.py:32
  19.8 17.9 %collective-permute-start.2 = (bf16[2,128,640]{2,1,0:T(8,128)(2,1)}, bf16[2,128,640]{2,1,0:T(8,128)(2,1)S(1)}, u32[]{:S(2)}, u32[]{:S(2)}) collective-permute-start(bf16[2,128,640]{2,1,0:T(8,128)(2,1)} %get-tuple-element.11.kv_own), channel_id=1, source_target_pairs={{0,4},{1,5},{2,6},{3,7},{4,8},{5,9},{6,10},{7,11},{8,12},{9,13},{1... | collective-permute-start | bytes 983048 | tf_op jit(solution)/shard_map/ppermute | solution.py:32
  24.4 13.3 %collective-permute-start.5 = (bf16[2,128,640]{2,1,0:T(8,128)(2,1)S(1)}, bf16[2,128,640]{2,1,0:T(8,128)(2,1)S(1)}, u32[]{:S(2)}, u32[]{:S(2)}) collective-permute-start(bf16[2,128,640]{2,1,0:T(8,128)(2,1)S(1)} %collective-permute-done.1.kv_pair), channel_id=1, source_target_pairs={{4,0},{5,1},{6,2},{7,3},{8,4},{9,5},{10,6},{11,7},{12,8},{13,9},{1... | collective-permute-start | bytes 983048 | tf_op jit(solution)/shard_map/ppermute | solution.py:32
  25.7 12.8 %collective-permute-start.3 = (bf16[2,128,640]{2,1,0:T(8,128)(2,1)S(1)}, bf16[2,128,640]{2,1,0:T(8,128)(2,1)S(1)}, u32[]{:S(2)}, u32[]{:S(2)}) collective-permute-start(bf16[2,128,640]{2,1,0:T(8,128)(2,1)S(1)} %collective-permute-done.1.kv_pair), channel_id=1, source_target_pairs={{0,4},{1,5},{2,6},{3,7},{4,8},{5,9},{6,10},{7,11},{8,12},{9,13},{1... | collective-permute-start | bytes 983048 | tf_op jit(solution)/shard_map/ppermute | solution.py:32
  30.3 7.4 %collective-permute-start = (bf16[128,640]{1,0:T(8,128)(2,1)}, bf16[128,640]{1,0:T(8,128)(2,1)S(1)}, u32[]{:S(2)}, u32[]{:S(2)}) collective-permute-start(bf16[128,640]{1,0:T(8,128)(2,1)} %get-tuple-element.10), channel_id=1, source_target_pairs={{0,2},{1,3},{2,0},{3,1},{4,6},{5,7},{6,4},{7,5},{8,10},{9,11},{10,... | collective-permute-start | bytes 491528 | tf_op jit(solution)/shard_map/ppermute | solution.py:32
  38.5 1.0 copy-start.4
  39.5 0.9 copy-start.5
  40.4 0.7 copy-start.6
  46.3 0.7 copy-start.7
  47.0 3.5 %copy-start.1 = (bf16[640,256]{1,0:T(8,128)(2,1)}, bf16[640,256]{1,0:T(8,128)(2,1)S(1)}, u32[]{:S(2)}) copy-start(bf16[640,256]{1,0:T(8,128)(2,1)S(1)} %get-tuple-element.13.attended.att) | copy-start | bytes 983044
  47.0 3.5 %collective-permute-start.7 = (bf16[640,256]{1,0:T(8,128)(2,1)S(1)}, bf16[640,256]{1,0:T(8,128)(2,1)S(1)}, u32[]{:S(2)}, u32[]{:S(2)}) collective-permute-start(bf16[640,256]{1,0:T(8,128)(2,1)S(1)} %get-tuple-element.13.attended.att), channel_id=1, source_target_pairs={{0,1},{1,0},{2,3},{3,2},{4,5},{5,4},{6,7},{7,6},{8,9},{9,8},{10,11... | collective-permute-start | bytes 983048 | tf_op jit(solution)/shard_map/ppermute | solution.py:32
  48.9 1.6 %copy-start.8 = (bf16[4,640,128]{2,1,0:T(8,128)(2,1)}, bf16[4,640,128]{2,1,0:T(8,128)(2,1)S(1)}, u32[]{:S(2)}) copy-start(bf16[4,640,128]{2,1,0:T(8,128)(2,1)S(1)} %all-to-all-done.exchanged) | copy-start | bytes 1966084
  50.5 0.7 copy-start.9
  54.1 65.9 %copy-start = (bf16[1280,1280]{1,0:T(8,128)(2,1)S(1)}, bf16[1280,1280]{1,0:T(8,128)(2,1)}, u32[]{:S(2)}) copy-start(bf16[1280,1280]{1,0:T(8,128)(2,1)} %weight.1) | copy-start | bytes 9830404
  107.4 16.5 %all-to-all-start.3 = ((bf16[24,24,128]{2,1,0:T(8,128)(2,1)}), bf16[24,24,128]{2,1,0:T(8,128)(2,1)S(1)}, u32[]{:S(2)}, u32[]{:S(2)}) async-start(bf16[24,24,128]{2,1,0:T(8,128)(2,1)} %shard_map.91), calls=%async_computation.3 | async-start | bytes 294912 | tf_op jit(solution)/shard_map/all_to_all | solution.py:356
  112.2 7.8 %collective-permute-start.6 = (bf16[640,128]{1,0:T(8,128)(2,1)}, bf16[640,128]{1,0:T(8,128)(2,1)S(1)}, u32[]{:S(2)}, u32[]{:S(2)}) collective-permute-start(bf16[640,128]{1,0:T(8,128)(2,1)} %copy-done.7), channel_id=1, source_target_pairs={{0,2},{1,3},{2,0},{3,1},{4,6},{5,7},{6,4},{7,5},{8,10},{9,11},{10,... | collective-permute-start | bytes 491528 | tf_op jit(solution)/shard_map/ppermute | solution.py:32
  120.0 1.0 copy-start.2
  121.0 1.0 copy-start.3

commit v3 on v2

--- a/solution.py
+++ b/solution.py
@@ -173,26 +173,29 @@
     )
 
 
-def first_sum_kernel(width, terms, out):
-    parts = out.shape[0] // (terms.shape[1] // width)
+def first_sum_kernel(terms, out):
+    out[...] = sum(terms[i].astype(jnp.float32) for i in range(terms.shape[0])).astype(
+        jnp.bfloat16
+    )
+
+
+def second_sum_kernel(terms, out):
+    total = sum(terms[i].astype(jnp.float32) for i in range(terms.shape[0]))
     tall = out.shape[1]
-    for block in range(terms.shape[1] // width):
-        some = slice(block * width, (block + 1) * width)
-        total = sum(terms[i, some, :].astype(jnp.float32) for i in range(terms.shape[0]))
-        for part in range(parts):
-            column, row = part // 2 * 128, part % 2 * tall
-            if column < terms.shape[2]:
-                tile = total[row : row + tall, column : column + 128]
-                if tile.shape[0] < tall:
-                    tile = jnp.concatenate(
-                        [tile, jnp.zeros((tall - tile.shape[0], 128), jnp.float32)], axis=0
-                    )
-            else:
-                tile = jnp.zeros((tall, 128), jnp.float32)
-            out[block * parts + part] = tile.astype(jnp.bfloat16)
-
-
-def second_sum_kernel(scale, terms, out):
+    for part in range(out.shape[0]):
+        column, row = part // 2 * 128, part % 2 * tall
+        if column < terms.shape[2]:
+            tile = total[row : row + tall, column : column + 128]
+            if tile.shape[0] < tall:
+                tile = jnp.concatenate(
+                    [tile, jnp.zeros((tall - tile.shape[0], 128), jnp.float32)], axis=0
+                )
+        else:
+            tile = jnp.zeros((tall, 128), jnp.float32)
+        out[part] = tile.astype(jnp.bfloat16)
+
+
+def third_sum_kernel(scale, terms, out):
     total = sum(terms[i].astype(jnp.float32) for i in range(terms.shape[0])) * scale
     total = total.astype(jnp.bfloat16)
     for i in range(out.shape[0]):
@@ -272,7 +275,9 @@
     kv_right_pair = to_previous(kv_pair)
     q_pair = to_pair(q_other)
     quads = [list(range(first, first + 4)) for first in range(0, 2 * seqs, 4)]
-    exchanged = lax.all_to_all(exchanged, ("seq", "dp"), 0, 0, tiled=True, axis_index_groups=quads)
+    exchanged = lax.all_to_all(
+        exchanged, ("seq", "dp"), 0, 0, tiled=True, axis_index_groups=quads
+    )
     attended, passed = call(
         functools.partial(attention_kernel, head_dim),
         (bf16(half, 2 * rows), bf16(half, rows)),
@@ -315,7 +320,6 @@
     groups = sections * cores
     grad_scale = 1.0 / float(groups * seqs * rows) ** 0.5
     side_x, side_y = 4, sections // 4
-    parts, tall = units, 24
     lines = [
         [(x * side_y + y) for x in range(side_x)] for y in range(side_y)
     ]
@@ -328,30 +332,37 @@
         axis_index_groups=lines,
     )
     terms = call(
-        functools.partial(first_sum_kernel, width),
-        bf16(side_y * parts, tall, 128),
+        first_sum_kernel,
+        bf16(side_y * width, half),
         [VMEM],
         half * half,
         3 * half * half,
     )(terms)
-    planes = [
-        [
-            ((x * side_y + y) * seqs + (first + part) * 2 + side) * cores + core
-            for y in range(side_y)
-            for part in range(parts)
-        ]
-        for x in range(side_x)
-        for first in range(0, units, parts)
-        for side in range(2)
-        for core in range(cores)
-    ]
-    terms = lax.all_to_all(terms, AXES, 0, 0, tiled=True, axis_index_groups=planes)
+    rows_of_chips = [[x * side_y + y for y in range(side_y)] for x in range(side_x)]
+    terms = lax.all_to_all(
+        terms.reshape(side_y, width, half),
+        "section",
+        0,
+        0,
+        tiled=True,
+        axis_index_groups=rows_of_chips,
+    )
+    tall = 24
+    terms = call(
+        second_sum_kernel,
+        bf16(units, tall, 128),
+        [VMEM],
+        side_y * width * half,
+        3 * side_y * width * half,
+    )(terms)
+    same_side = [list(range(side, seqs, 2)) for side in range(2)]
+    terms = lax.all_to_all(terms, "seq", 0, 0, tiled=True, axis_index_groups=same_side)
     spread = call(
-        functools.partial(second_sum_kernel, grad_scale),
+        functools.partial(third_sum_kernel, grad_scale),
         bf16(seqs, tall, 128),
         [VMEM],
-        side_y * parts * tall * 128,
-        2 * (side_y * parts + seqs) * tall * 128,
+        units * tall * 128,
+        2 * (units + seqs) * tall * 128,
     )(terms)
     spread = lax.all_to_all(spread, "seq", 0, 0, tiled=True)
     weight_grad = call(

time: 125 us -> 126 us (level)
  blocking collectives: 52.5 us -> 54.1 us
    all_to_all x1 -> x2, blocking collectives: 35.5 us -> 37.2 us  [the longest x1 25.2 us: per_device(): lax.all_to_all(terms, 'seq', 0, 0, tiled=True, axis_index_groups=same_side)]
where the time goes in v3:
time: 126 us
  blocking collectives  54.1 us (43%)
  starting transfers between devices  36.8 us (29%)
  Pallas kernels  14.6 us (12%)
  waiting for transfers between devices  13.4 us (11%)
  local copies, waits for them, and re-layouts  5.93 us (5%)
    ppermute x8, starting transfers between devices, moved(): return lax.ppermute(value, AXES, pairs)  29.1 us
    all_to_all x1, blocking collectives, per_device(): lax.all_to_all(terms, 'seq', 0, 0, tiled=True, axis_index_groups=same_side)  25.2 us
    all_to_all x1, blocking collectives, per_device(): lax.all_to_all(partial.reshape(side_x, side_y * width, half), 'section',...  16.9 us
    ppermute x8, waiting for transfers between devices, moved(): return lax.ppermute(value, AXES, pairs)  13.4 us
    all_to_all x1, blocking collectives, per_device(): lax.all_to_all(terms.reshape(side_y, width, half), 'section', 0, 0, tiled...  11.9 us
    unnamed x20, local copies, waits for them, and re-layouts  5.93 us
    pallas_call x1, Pallas kernels, per_device(): call(functools.partial(attention_kernel, head_dim), (bf16(half, 2 * rows)...  5.22 us
    all_to_all x1, starting transfers between devices, per_device(): spread = lax.all_to_all(spread, 'seq', 0, 0, tiled=True)  4.2 us
  transfers between devices with their start and end apart: 10, of which 4 were waited for; matrix products, arithmetic and copies ran while one was open for 0% of the time, Pallas kernels for 6%

profile of v3, /device:TPU:8, one launch (start us, length us, event | category | flops | bytes accessed | tf_op | source)
XLA Modules:
  0.0 125.5 jit_solution(2696076513040458610)
XLA Ops:
  0.6 3.0 %shard_map.86 = (bf16[2,128,640]{2,1,0:T(8,128)(2,1)}, bf16[2,128,640]{2,1,0:T(8,128)(2,1)}, bf16[128,640]{1,0:T(8,128)(2,1)}, bf16[128,640]{1,0:T(8,128)(2,1)}, bf16[4,640,128]{2,1,0:T(8,128)(2,1)}) custom-call(s32[1]{0:T(128)} %bitcast.place, bf16[128,1280]{1,0:T(8,128)(2,1)} %bitcast.13, bf16[128,1280]{1,0:T(8,128)(2,1)} %bitcast.14, ...), custom_call_target="tpu_custom_call" | custom-call | flops 209715200 | bytes 3932160 | tf_op jit(solution)/shard_map/pallas_call | solution.py:257
  3.7 11.3 %collective-permute-start.1 = (bf16[2,128,640]{2,1,0:T(8,128)(2,1)}, bf16[2,128,640]{2,1,0:T(8,128)(2,1)S(1)}, u32[]{:S(2)}, u32[]{:S(2)}) collective-permute-start(bf16[2,128,640]{2,1,0:T(8,128)(2,1)} %get-tuple-element.12), channel_id=1, source_target_pairs={{0,2},{1,3},{2,0},{3,1},{4,6},{5,7},{6,4},{7,5},{8,10},{9,11},{10,... | collective-permute-start | bytes 983048 | tf_op jit(solution)/shard_map/ppermute | solution.py:32
  15.0 3.5 %all-to-all-start = ((bf16[4,640,128]{2,1,0:T(8,128)(2,1)}), bf16[4,640,128]{2,1,0:T(8,128)(2,1)S(1)}, u32[]{:S(2)}, u32[]{:S(2)}) async-start(bf16[4,640,128]{2,1,0:T(8,128)(2,1)} %get-tuple-element.15), calls=%async_computation | async-start | bytes 1310720 | tf_op jit(solution)/shard_map/all_to_all | solution.py:278
  18.5 1.3 %collective-permute-start.4 = (bf16[2,128,640]{2,1,0:T(8,128)(2,1)}, bf16[2,128,640]{2,1,0:T(8,128)(2,1)S(1)}, u32[]{:S(2)}, u32[]{:S(2)}) collective-permute-start(bf16[2,128,640]{2,1,0:T(8,128)(2,1)} %get-tuple-element.11.kv_own), channel_id=1, source_target_pairs={{4,0},{5,1},{6,2},{7,3},{8,4},{9,5},{10,6},{11,7},{12,8},{13,9},{1... | collective-permute-start | bytes 983048 | tf_op jit(solution)/shard_map/ppermute | solution.py:32
  19.8 4.6 %collective-permute-start.2 = (bf16[2,128,640]{2,1,0:T(8,128)(2,1)}, bf16[2,128,640]{2,1,0:T(8,128)(2,1)S(1)}, u32[]{:S(2)}, u32[]{:S(2)}) collective-permute-start(bf16[2,128,640]{2,1,0:T(8,128)(2,1)} %get-tuple-element.11.kv_own), channel_id=1, source_target_pairs={{0,4},{1,5},{2,6},{3,7},{4,8},{5,9},{6,10},{7,11},{8,12},{9,13},{1... | collective-permute-start | bytes 983048 | tf_op jit(solution)/shard_map/ppermute | solution.py:32
  24.4 1.3 %collective-permute-start.5 = (bf16[2,128,640]{2,1,0:T(8,128)(2,1)S(1)}, bf16[2,128,640]{2,1,0:T(8,128)(2,1)S(1)}, u32[]{:S(2)}, u32[]{:S(2)}) collective-permute-start(bf16[2,128,640]{2,1,0:T(8,128)(2,1)S(1)} %collective-permute-done.1.kv_pair), channel_id=1, source_target_pairs={{4,0},{5,1},{6,2},{7,3},{8,4},{9,5},{10,6},{11,7},{12,8},{13,9},{1... | collective-permute-start | bytes 983048 | tf_op jit(solution)/shard_map/ppermute | solution.py:32
  25.7 4.6 %collective-permute-start.3 = (bf16[2,128,640]{2,1,0:T(8,128)(2,1)S(1)}, bf16[2,128,640]{2,1,0:T(8,128)(2,1)S(1)}, u32[]{:S(2)}, u32[]{:S(2)}) collective-permute-start(bf16[2,128,640]{2,1,0:T(8,128)(2,1)S(1)} %collective-permute-done.1.kv_pair), channel_id=1, source_target_pairs={{0,4},{1,5},{2,6},{3,7},{4,8},{5,9},{6,10},{7,11},{8,12},{9,13},{1... | collective-permute-start | bytes 983048 | tf_op jit(solution)/shard_map/ppermute | solution.py:32
  30.3 1.9 %collective-permute-start = (bf16[128,640]{1,0:T(8,128)(2,1)}, bf16[128,640]{1,0:T(8,128)(2,1)S(1)}, u32[]{:S(2)}, u32[]{:S(2)}) collective-permute-start(bf16[128,640]{1,0:T(8,128)(2,1)} %get-tuple-element.10), channel_id=1, source_target_pairs={{0,2},{1,3},{2,0},{3,1},{4,6},{5,7},{6,4},{7,5},{8,10},{9,11},{10,... | collective-permute-start | bytes 491528 | tf_op jit(solution)/shard_map/ppermute | solution.py:32
  32.2 5.5 %collective-permute-done.q_pair = bf16[128,640]{1,0:T(8,128)(2,1)S(1)} collective-permute-done((bf16[128,640]{1,0:T(8,128)(2,1)}, bf16[128,640]{1,0:T(8,128)(2,1)S(1)}, u32[]{:S(2)}, u32[]{:S(2)}) %collective-permute-start) | collective-permute-done | bytes 163872 | tf_op jit(solution)/shard_map/ppermute | solution.py:32
  37.7 0.8 collective-permute-done.3.kv_left_pair
  38.5 1.0 copy-done.4
  39.5 0.9 copy-done.5
  40.4 0.7 copy-done.6
  41.1 5.2 %shard_map.87 = (bf16[640,256]{1,0:T(8,128)(2,1)S(1)}, bf16[640,128]{1,0:T(8,128)(2,1)S(1)}) custom-call(s32[1]{0:T(128)} %bitcast.place, s32[1,3072]{1,0:T(1,128)S(1)} %copy-done.6, bf16[128,640]{1,0:T(8,128)(2,1)S(1)} %copy-done.5, bf16[128,640]{1,0:T(8,128)(2,1)S(1)} %collective-permute-done.q_pair, bf16[2,128,640]{2,1,0:T(8,128)(2,1)S(1)} %copy-done.4, ...), custom_call_target="tpu_custom_call" | custom-call | flops 503316480 | bytes 2129920 | tf_op jit(solution)/shard_map/pallas_call | solution.py:281
  46.3 0.0 copy-start.7
  46.3 0.7 copy-done.7
  47.0 1.9 %collective-permute-start.7 = (bf16[640,256]{1,0:T(8,128)(2,1)S(1)}, bf16[640,256]{1,0:T(8,128)(2,1)S(1)}, u32[]{:S(2)}, u32[]{:S(2)}) collective-permute-start(bf16[640,256]{1,0:T(8,128)(2,1)S(1)} %get-tuple-element.13.attended.att), channel_id=1, source_target_pairs={{0,1},{1,0},{2,3},{3,2},{4,5},{5,4},{6,7},{7,6},{8,9},{9,8},{10,11... | collective-permute-start | bytes 983048 | tf_op jit(solution)/shard_map/ppermute | solution.py:32
  48.9 1.6 %collective-permute-done.7.att_core = bf16[640,256]{1,0:T(8,128)(2,1)S(1)} collective-permute-done((bf16[640,256]{1,0:T(8,128)(2,1)S(1)}, bf16[640,256]{1,0:T(8,128)(2,1)S(1)}, u32[]{:S(2)}, u32[]{:S(2)}) %collective-permute-start.7) | collective-permute-done | bytes 327712 | tf_op jit(solution)/shard_map/ppermute | solution.py:32
  50.5 0.7 copy-done.9
  51.2 2.9 %shard_map.89 = bf16[640,640]{1,0:T(8,128)(2,1)} custom-call(s32[1]{0:T(128)} %bitcast.place, bf16[640,256]{1,0:T(8,128)(2,1)} %copy-done.1, bf16[640,256]{1,0:T(8,128)(2,1)} %copy-done.9, bf16[4,640,128]{2,1,0:T(8,128)(2,1)} %copy-done.8), custom_call_target="tpu_custom_call" | custom-call | flops 419430400 | bytes 819200 | tf_op jit(solution)/shard_map/pallas_call | solution.py:303
  54.1 16.9 %all_to_all.25.terms = bf16[4,160,640]{2,1,0:T(8,128)(2,1)S(1)} all-to-all(bf16[4,160,640]{2,1,0:T(8,128)(2,1)} %bitcast.11), channel_id=1, replica_groups={{0,192,384,576},{48,240,432,624},{96,288,480,672},{144,336,528,720},{1,..., dimensions={0} | all-to-all | bytes 1638400 | tf_op jit(solution)/shard_map/all_to_all | solution.py:326
  71.1 0.1 shard_map.90
  71.2 11.9 %all_to_all.26.terms = bf16[4,40,640]{2,1,0:T(8,128)(2,1)S(1)} all-to-all(bf16[4,40,640]{2,1,0:T(8,128)(2,1)S(1)} %bitcast.9), channel_id=1, replica_groups={{0,48,96,144},{192,240,288,336},{384,432,480,528},{576,624,672,720},{1,..., dimensions={0} | all-to-all | bytes 409600 | tf_op jit(solution)/shard_map/all_to_all | solution.py:342
  83.2 25.2 %all_to_all.27.terms = bf16[12,24,128]{2,1,0:T(8,128)(2,1)S(1)} all-to-all(bf16[12,24,128]{2,1,0:T(8,128)(2,1)S(1)} %shard_map.91), channel_id=1, replica_groups={{0,4,8,12,16,20,24,28,32,36,40,44},{2,6,10,14,18,22,26,30,34,38,42,46},..., dimensions={0} | all-to-all | bytes 147456 | tf_op jit(solution)/shard_map/all_to_all | solution.py:359
  108.4 0.7 shard_map.92
  109.1 4.2 %all-to-all-start.4 = ((bf16[24,24,128]{2,1,0:T(8,128)(2,1)}), bf16[24,24,128]{2,1,0:T(8,128)(2,1)S(1)}, u32[]{:S(2)}, u32[]{:S(2)}) async-start(bf16[24,24,128]{2,1,0:T(8,128)(2,1)} %shard_map.92), calls=%async_computation.4 | async-start | bytes 294912 | tf_op jit(solution)/shard_map/all_to_all | solution.py:367
  113.3 2.2 %collective-permute-start.6 = (bf16[640,128]{1,0:T(8,128)(2,1)}, bf16[640,128]{1,0:T(8,128)(2,1)S(1)}, u32[]{:S(2)}, u32[]{:S(2)}) collective-permute-start(bf16[640,128]{1,0:T(8,128)(2,1)} %copy-done.7), channel_id=1, source_target_pairs={{0,2},{1,3},{2,0},{3,1},{4,6},{5,7},{6,4},{7,5},{8,10},{9,11},{10,... | collective-permute-start | bytes 491528 | tf_op jit(solution)/shard_map/ppermute | solution.py:32
  115.5 5.5 %collective-permute-done.6.received = bf16[640,128]{1,0:T(8,128)(2,1)S(1)} collective-permute-done((bf16[640,128]{1,0:T(8,128)(2,1)}, bf16[640,128]{1,0:T(8,128)(2,1)S(1)}, u32[]{:S(2)}, u32[]{:S(2)}) %collective-permute-start.6) | collective-permute-done | bytes 163872 | tf_op jit(solution)/shard_map/ppermute | solution.py:32
  121.0 1.0 copy-done.2
  122.0 1.0 copy-done.3
  122.9 1.9 %shard_map.88 = bf16[128,1280]{1,0:T(8,128)(2,1)} custom-call(s32[1]{0:T(128)} %bitcast.place, bf16[640,256]{1,0:T(8,128)(2,1)S(1)} %copy-done.2, bf16[640,128]{1,0:T(8,128)(2,1)S(1)} %collective-permute-done.6.received, bf16[1280,1280]{1,0:T(8,128)(2,1)S(1)} %copy-done, bf16[128,1280]{1,0:T(8,128)(2,1)S(1)} %bitcast.10), custom_call_target="tpu_custom_call" | custom-call | flops 419430400 | bytes 3276800 | tf_op jit(solution)/shard_map/pallas_call | solution.py:311
  124.8 0.7 shard_map.93
  (19 shorter events, 0.1 us)
Async XLA Ops:
  3.7 20.7 %collective-permute-start.1 = (bf16[2,128,640]{2,1,0:T(8,128)(2,1)}, bf16[2,128,640]{2,1,0:T(8,128)(2,1)S(1)}, u32[]{:S(2)}, u32[]{:S(2)}) collective-permute-start(bf16[2,128,640]{2,1,0:T(8,128)(2,1)} %get-tuple-element.12), channel_id=1, source_target_pairs={{0,2},{1,3},{2,0},{3,1},{4,6},{5,7},{6,4},{7,5},{8,10},{9,11},{10,... | collective-permute-start | bytes 983048 | tf_op jit(solution)/shard_map/ppermute | solution.py:32
  15.0 33.9 %all-to-all-start = ((bf16[4,640,128]{2,1,0:T(8,128)(2,1)}), bf16[4,640,128]{2,1,0:T(8,128)(2,1)S(1)}, u32[]{:S(2)}, u32[]{:S(2)}) async-start(bf16[4,640,128]{2,1,0:T(8,128)(2,1)} %get-tuple-element.15), calls=%async_computation | async-start | bytes 1310720 | tf_op jit(solution)/shard_map/all_to_all | solution.py:278
  18.5 19.2 %collective-permute-start.4 = (bf16[2,128,640]{2,1,0:T(8,128)(2,1)}, bf16[2,128,640]{2,1,0:T(8,128)(2,1)S(1)}, u32[]{:S(2)}, u32[]{:S(2)}) collective-permute-start(bf16[2,128,640]{2,1,0:T(8,128)(2,1)} %get-tuple-element.11.kv_own), channel_id=1, source_target_pairs={{4,0},{5,1},{6,2},{7,3},{8,4},{9,5},{10,6},{11,7},{12,8},{13,9},{1... | collective-permute-start | bytes 983048 | tf_op jit(solution)/shard_map/ppermute | solution.py:32
  19.8 17.9 %collective-permute-start.2 = (bf16[2,128,640]{2,1,0:T(8,128)(2,1)}, bf16[2,128,640]{2,1,0:T(8,128)(2,1)S(1)}, u32[]{:S(2)}, u32[]{:S(2)}) collective-permute-start(bf16[2,128,640]{2,1,0:T(8,128)(2,1)} %get-tuple-element.11.kv_own), channel_id=1, source_target_pairs={{0,4},{1,5},{2,6},{3,7},{4,8},{5,9},{6,10},{7,11},{8,12},{9,13},{1... | collective-permute-start | bytes 983048 | tf_op jit(solution)/shard_map/ppermute | solution.py:32
  24.4 13.3 %collective-permute-start.5 = (bf16[2,128,640]{2,1,0:T(8,128)(2,1)S(1)}, bf16[2,128,640]{2,1,0:T(8,128)(2,1)S(1)}, u32[]{:S(2)}, u32[]{:S(2)}) collective-permute-start(bf16[2,128,640]{2,1,0:T(8,128)(2,1)S(1)} %collective-permute-done.1.kv_pair), channel_id=1, source_target_pairs={{4,0},{5,1},{6,2},{7,3},{8,4},{9,5},{10,6},{11,7},{12,8},{13,9},{1... | collective-permute-start | bytes 983048 | tf_op jit(solution)/shard_map/ppermute | solution.py:32
  25.7 12.8 %collective-permute-start.3 = (bf16[2,128,640]{2,1,0:T(8,128)(2,1)S(1)}, bf16[2,128,640]{2,1,0:T(8,128)(2,1)S(1)}, u32[]{:S(2)}, u32[]{:S(2)}) collective-permute-start(bf16[2,128,640]{2,1,0:T(8,128)(2,1)S(1)} %collective-permute-done.1.kv_pair), channel_id=1, source_target_pairs={{0,4},{1,5},{2,6},{3,7},{4,8},{5,9},{6,10},{7,11},{8,12},{9,13},{1... | collective-permute-start | bytes 983048 | tf_op jit(solution)/shard_map/ppermute | solution.py:32
  30.3 7.4 %collective-permute-start = (bf16[128,640]{1,0:T(8,128)(2,1)}, bf16[128,640]{1,0:T(8,128)(2,1)S(1)}, u32[]{:S(2)}, u32[]{:S(2)}) collective-permute-start(bf16[128,640]{1,0:T(8,128)(2,1)} %get-tuple-element.10), channel_id=1, source_target_pairs={{0,2},{1,3},{2,0},{3,1},{4,6},{5,7},{6,4},{7,5},{8,10},{9,11},{10,... | collective-permute-start | bytes 491528 | tf_op jit(solution)/shard_map/ppermute | solution.py:32
  38.5 1.0 copy-start.4
  39.5 0.9 copy-start.5
  40.4 0.7 copy-start.6
  46.3 0.7 copy-start.7
  47.0 3.5 %copy-start.1 = (bf16[640,256]{1,0:T(8,128)(2,1)}, bf16[640,256]{1,0:T(8,128)(2,1)S(1)}, u32[]{:S(2)}) copy-start(bf16[640,256]{1,0:T(8,128)(2,1)S(1)} %get-tuple-element.13.attended.att) | copy-start | bytes 983044
  47.0 3.5 %collective-permute-start.7 = (bf16[640,256]{1,0:T(8,128)(2,1)S(1)}, bf16[640,256]{1,0:T(8,128)(2,1)S(1)}, u32[]{:S(2)}, u32[]{:S(2)}) collective-permute-start(bf16[640,256]{1,0:T(8,128)(2,1)S(1)} %get-tuple-element.13.attended.att), channel_id=1, source_target_pairs={{0,1},{1,0},{2,3},{3,2},{4,5},{5,4},{6,7},{7,6},{8,9},{9,8},{10,11... | collective-permute-start | bytes 983048 | tf_op jit(solution)/shard_map/ppermute | solution.py:32
  48.9 1.6 %copy-start.8 = (bf16[4,640,128]{2,1,0:T(8,128)(2,1)}, bf16[4,640,128]{2,1,0:T(8,128)(2,1)S(1)}, u32[]{:S(2)}) copy-start(bf16[4,640,128]{2,1,0:T(8,128)(2,1)S(1)} %all-to-all-done.exchanged) | copy-start | bytes 1966084
  50.5 0.7 copy-start.9
  54.1 66.9 %copy-start = (bf16[1280,1280]{1,0:T(8,128)(2,1)S(1)}, bf16[1280,1280]{1,0:T(8,128)(2,1)}, u32[]{:S(2)}) copy-start(bf16[1280,1280]{1,0:T(8,128)(2,1)} %weight.1) | copy-start | bytes 9830404
  109.1 15.8 %all-to-all-start.4 = ((bf16[24,24,128]{2,1,0:T(8,128)(2,1)}), bf16[24,24,128]{2,1,0:T(8,128)(2,1)S(1)}, u32[]{:S(2)}, u32[]{:S(2)}) async-start(bf16[24,24,128]{2,1,0:T(8,128)(2,1)} %shard_map.92), calls=%async_computation.4 | async-start | bytes 294912 | tf_op jit(solution)/shard_map/all_to_all | solution.py:367
  113.3 7.7 %collective-permute-start.6 = (bf16[640,128]{1,0:T(8,128)(2,1)}, bf16[640,128]{1,0:T(8,128)(2,1)S(1)}, u32[]{:S(2)}, u32[]{:S(2)}) collective-permute-start(bf16[640,128]{1,0:T(8,128)(2,1)} %copy-done.7), channel_id=1, source_target_pairs={{0,2},{1,3},{2,0},{3,1},{4,6},{5,7},{6,4},{7,5},{8,10},{9,11},{10,... | collective-permute-start | bytes 491528 | tf_op jit(solution)/shard_map/ppermute | solution.py:32
  121.0 1.0 copy-start.2
  122.0 1.0 copy-start.3

commit v4 on v3

--- a/solution.py
+++ b/solution.py
@@ -174,12 +174,6 @@
 
 
 def first_sum_kernel(terms, out):
-    out[...] = sum(terms[i].astype(jnp.float32) for i in range(terms.shape[0])).astype(
-        jnp.bfloat16
-    )
-
-
-def second_sum_kernel(terms, out):
     total = sum(terms[i].astype(jnp.float32) for i in range(terms.shape[0]))
     tall = out.shape[1]
     for part in range(out.shape[0]):
@@ -195,7 +189,7 @@
         out[part] = tile.astype(jnp.bfloat16)
 
 
-def third_sum_kernel(scale, terms, out):
+def second_sum_kernel(scale, terms, out):
     total = sum(terms[i].astype(jnp.float32) for i in range(terms.shape[0])) * scale
     total = total.astype(jnp.bfloat16)
     for i in range(out.shape[0]):
@@ -319,46 +313,21 @@
 
     groups = sections * cores
     grad_scale = 1.0 / float(groups * seqs * rows) ** 0.5
-    side_x, side_y = 4, sections // 4
-    lines = [
-        [(x * side_y + y) for x in range(side_x)] for y in range(side_y)
-    ]
     terms = lax.all_to_all(
-        partial.reshape(side_x, side_y * width, half),
-        "section",
-        0,
-        0,
-        tiled=True,
-        axis_index_groups=lines,
-    )
+        partial.reshape(sections, width, half), "section", 0, 0, tiled=True
+    )
+    tall = 24
     terms = call(
         first_sum_kernel,
-        bf16(side_y * width, half),
-        [VMEM],
-        half * half,
-        3 * half * half,
-    )(terms)
-    rows_of_chips = [[x * side_y + y for y in range(side_y)] for x in range(side_x)]
-    terms = lax.all_to_all(
-        terms.reshape(side_y, width, half),
-        "section",
-        0,
-        0,
-        tiled=True,
-        axis_index_groups=rows_of_chips,
-    )
-    tall = 24
-    terms = call(
-        second_sum_kernel,
         bf16(units, tall, 128),
         [VMEM],
-        side_y * width * half,
-        3 * side_y * width * half,
+        sections * width * half,
+        3 * sections * width * half,
     )(terms)
     same_side = [list(range(side, seqs, 2)) for side in range(2)]
     terms = lax.all_to_all(terms, "seq", 0, 0, tiled=True, axis_index_groups=same_side)
     spread = call(
-        functools.partial(third_sum_kernel, grad_scale),
+        functools.partial(second_sum_kernel, grad_scale),
         bf16(seqs, tall, 128),
         [VMEM],
         units * tall * 128,

time: 126 us -> 126 us (level)
    unnamed x20 -> x18, local copies, waits for them, and re-layouts: 5.93 us -> 5.26 us
    all_to_all x2 -> x1, blocking collectives: 28.9 us -> 29.1 us  [per_device(): lax.all_to_all(partial.reshape(sections, width, half), 'section', 0, 0, t...]
where the time goes in v4:
time: 126 us; the launch traced here: 125 us
  blocking collectives  54.5 us (43%)
  starting transfers between devices  36.8 us (29%)
  Pallas kernels  14.6 us (12%)
  waiting for transfers between devices  13.4 us (11%)
  local copies, waits for them, and re-layouts  5.26 us (4%)
    all_to_all x1, blocking collectives, per_device(): lax.all_to_all(partial.reshape(sections, width, half), 'section', 0, 0, t...  29.1 us
    ppermute x8, starting transfers between devices, moved(): return lax.ppermute(value, AXES, pairs)  29 us
    all_to_all x1, blocking collectives, per_device(): lax.all_to_all(terms, 'seq', 0, 0, tiled=True, axis_index_groups=same_side)  25.5 us
    ppermute x8, waiting for transfers between devices, moved(): return lax.ppermute(value, AXES, pairs)  13.4 us
    unnamed x18, local copies, waits for them, and re-layouts  5.26 us
    pallas_call x1, Pallas kernels, per_device(): call(functools.partial(attention_kernel, head_dim), (bf16(half, 2 * rows)...  5.23 us
    all_to_all x1, starting transfers between devices, per_device(): spread = lax.all_to_all(spread, 'seq', 0, 0, tiled=True)  4.35 us
    all_to_all x1, starting transfers between devices, per_device(): lax.all_to_all(exchanged, ('seq', 'dp'), 0, 0, tiled=True, axis_index_gro...  3.48 us
  transfers between devices with their start and end apart: 10, of which 4 were waited for; matrix products, arithmetic and copies ran while one was open for 0% of the time, Pallas kernels for 6%

profile of v4, /device:TPU:8, one launch (start us, length us, event | category | flops | bytes accessed | tf_op | source)
XLA Modules:
  0.0 125.3 jit_solution(11571093327764286912)
XLA Ops:
  0.6 3.0 %shard_map.86 = (bf16[2,128,640]{2,1,0:T(8,128)(2,1)}, bf16[2,128,640]{2,1,0:T(8,128)(2,1)}, bf16[128,640]{1,0:T(8,128)(2,1)}, bf16[128,640]{1,0:T(8,128)(2,1)}, bf16[4,640,128]{2,1,0:T(8,128)(2,1)}) custom-call(s32[1]{0:T(128)} %bitcast.place, bf16[128,1280]{1,0:T(8,128)(2,1)} %bitcast.11, bf16[128,1280]{1,0:T(8,128)(2,1)} %bitcast.12, ...), custom_call_target="tpu_custom_call" | custom-call | flops 209715200 | bytes 3932160 | tf_op jit(solution)/shard_map/pallas_call | solution.py:251
  3.7 11.3 %collective-permute-start.1 = (bf16[2,128,640]{2,1,0:T(8,128)(2,1)}, bf16[2,128,640]{2,1,0:T(8,128)(2,1)S(1)}, u32[]{:S(2)}, u32[]{:S(2)}) collective-permute-start(bf16[2,128,640]{2,1,0:T(8,128)(2,1)} %get-tuple-element.12), channel_id=1, source_target_pairs={{0,2},{1,3},{2,0},{3,1},{4,6},{5,7},{6,4},{7,5},{8,10},{9,11},{10,... | collective-permute-start | bytes 983048 | tf_op jit(solution)/shard_map/ppermute | solution.py:32
  15.0 3.5 %all-to-all-start = ((bf16[4,640,128]{2,1,0:T(8,128)(2,1)}), bf16[4,640,128]{2,1,0:T(8,128)(2,1)S(1)}, u32[]{:S(2)}, u32[]{:S(2)}) async-start(bf16[4,640,128]{2,1,0:T(8,128)(2,1)} %get-tuple-element.15), calls=%async_computation | async-start | bytes 1310720 | tf_op jit(solution)/shard_map/all_to_all | solution.py:272
  18.5 1.3 %collective-permute-start.4 = (bf16[2,128,640]{2,1,0:T(8,128)(2,1)}, bf16[2,128,640]{2,1,0:T(8,128)(2,1)S(1)}, u32[]{:S(2)}, u32[]{:S(2)}) collective-permute-start(bf16[2,128,640]{2,1,0:T(8,128)(2,1)} %get-tuple-element.11.kv_own), channel_id=1, source_target_pairs={{4,0},{5,1},{6,2},{7,3},{8,4},{9,5},{10,6},{11,7},{12,8},{13,9},{1... | collective-permute-start | bytes 983048 | tf_op jit(solution)/shard_map/ppermute | solution.py:32
  19.8 4.6 %collective-permute-start.2 = (bf16[2,128,640]{2,1,0:T(8,128)(2,1)}, bf16[2,128,640]{2,1,0:T(8,128)(2,1)S(1)}, u32[]{:S(2)}, u32[]{:S(2)}) collective-permute-start(bf16[2,128,640]{2,1,0:T(8,128)(2,1)} %get-tuple-element.11.kv_own), channel_id=1, source_target_pairs={{0,4},{1,5},{2,6},{3,7},{4,8},{5,9},{6,10},{7,11},{8,12},{9,13},{1... | collective-permute-start | bytes 983048 | tf_op jit(solution)/shard_map/ppermute | solution.py:32
  24.4 0.0 collective-permute-done.1.kv_pair
  24.4 1.3 %collective-permute-start.5 = (bf16[2,128,640]{2,1,0:T(8,128)(2,1)S(1)}, bf16[2,128,640]{2,1,0:T(8,128)(2,1)S(1)}, u32[]{:S(2)}, u32[]{:S(2)}) collective-permute-start(bf16[2,128,640]{2,1,0:T(8,128)(2,1)S(1)} %collective-permute-done.1.kv_pair), channel_id=1, source_target_pairs={{4,0},{5,1},{6,2},{7,3},{8,4},{9,5},{10,6},{11,7},{12,8},{13,9},{1... | collective-permute-start | bytes 983048 | tf_op jit(solution)/shard_map/ppermute | solution.py:32
  25.7 4.6 %collective-permute-start.3 = (bf16[2,128,640]{2,1,0:T(8,128)(2,1)S(1)}, bf16[2,128,640]{2,1,0:T(8,128)(2,1)S(1)}, u32[]{:S(2)}, u32[]{:S(2)}) collective-permute-start(bf16[2,128,640]{2,1,0:T(8,128)(2,1)S(1)} %collective-permute-done.1.kv_pair), channel_id=1, source_target_pairs={{0,4},{1,5},{2,6},{3,7},{4,8},{5,9},{6,10},{7,11},{8,12},{9,13},{1... | collective-permute-start | bytes 983048 | tf_op jit(solution)/shard_map/ppermute | solution.py:32
  30.3 1.9 %collective-permute-start = (bf16[128,640]{1,0:T(8,128)(2,1)}, bf16[128,640]{1,0:T(8,128)(2,1)S(1)}, u32[]{:S(2)}, u32[]{:S(2)}) collective-permute-start(bf16[128,640]{1,0:T(8,128)(2,1)} %get-tuple-element.10), channel_id=1, source_target_pairs={{0,2},{1,3},{2,0},{3,1},{4,6},{5,7},{6,4},{7,5},{8,10},{9,11},{10,... | collective-permute-start | bytes 491528 | tf_op jit(solution)/shard_map/ppermute | solution.py:32
  32.2 5.5 %collective-permute-done.q_pair = bf16[128,640]{1,0:T(8,128)(2,1)S(1)} collective-permute-done((bf16[128,640]{1,0:T(8,128)(2,1)}, bf16[128,640]{1,0:T(8,128)(2,1)S(1)}, u32[]{:S(2)}, u32[]{:S(2)}) %collective-permute-start) | collective-permute-done | bytes 163872 | tf_op jit(solution)/shard_map/ppermute | solution.py:32
  37.7 0.0 collective-permute-done.5.kv_right_pair
  37.7 0.8 collective-permute-done.3.kv_left_pair
  38.5 1.0 copy-done.4
  39.5 0.9 copy-done.5
  40.4 0.7 copy-done.6
  41.1 5.2 %shard_map.87 = (bf16[640,256]{1,0:T(8,128)(2,1)S(1)}, bf16[640,128]{1,0:T(8,128)(2,1)S(1)}) custom-call(s32[1]{0:T(128)} %bitcast.place, s32[1,3072]{1,0:T(1,128)S(1)} %copy-done.6, bf16[128,640]{1,0:T(8,128)(2,1)S(1)} %copy-done.5, bf16[128,640]{1,0:T(8,128)(2,1)S(1)} %collective-permute-done.q_pair, bf16[2,128,640]{2,1,0:T(8,128)(2,1)S(1)} %copy-done.4, ...), custom_call_target="tpu_custom_call" | custom-call | flops 503316480 | bytes 2129920 | tf_op jit(solution)/shard_map/pallas_call | solution.py:275
  46.4 0.0 copy-start.1
  46.4 1.9 %collective-permute-start.7 = (bf16[640,256]{1,0:T(8,128)(2,1)S(1)}, bf16[640,256]{1,0:T(8,128)(2,1)S(1)}, u32[]{:S(2)}, u32[]{:S(2)}) collective-permute-start(bf16[640,256]{1,0:T(8,128)(2,1)S(1)} %get-tuple-element.13.attended.att), channel_id=1, source_target_pairs={{0,1},{1,0},{2,3},{3,2},{4,5},{5,4},{6,7},{7,6},{8,9},{9,8},{10,11... | collective-permute-start | bytes 983048 | tf_op jit(solution)/shard_map/ppermute | solution.py:32
  48.3 0.0 all-to-all-done.exchanged
  48.3 1.6 %collective-permute-done.7.att_core = bf16[640,256]{1,0:T(8,128)(2,1)S(1)} collective-permute-done((bf16[640,256]{1,0:T(8,128)(2,1)S(1)}, bf16[640,256]{1,0:T(8,128)(2,1)S(1)}, u32[]{:S(2)}, u32[]{:S(2)}) %collective-permute-start.7) | collective-permute-done | bytes 327712 | tf_op jit(solution)/shard_map/ppermute | solution.py:32
  49.9 0.7 copy-done.8
  50.6 2.9 %shard_map.89 = bf16[640,640]{1,0:T(8,128)(2,1)} custom-call(s32[1]{0:T(128)} %bitcast.place, bf16[640,256]{1,0:T(8,128)(2,1)} %copy-done.1, bf16[640,256]{1,0:T(8,128)(2,1)} %copy-done.8, bf16[4,640,128]{2,1,0:T(8,128)(2,1)} %copy-done.7), custom_call_target="tpu_custom_call" | custom-call | flops 419430400 | bytes 819200 | tf_op jit(solution)/shard_map/pallas_call | solution.py:297
  53.5 29.1 %all_to_all.20.terms = bf16[16,40,640]{2,1,0:T(8,128)(2,1)S(1)} all-to-all(bf16[16,40,640]{2,1,0:T(8,128)(2,1)} %bitcast.9), channel_id=1, replica_groups=mesh['section'=16,'seq'=24,'dp'=2] {'section'}, dimensions={0} | all-to-all | bytes 1638400 | tf_op jit(solution)/shard_map/all_to_all | solution.py:316
  82.6 0.1 shard_map.90
  82.7 25.5 %all_to_all.21.terms = bf16[12,24,128]{2,1,0:T(8,128)(2,1)S(1)} all-to-all(bf16[12,24,128]{2,1,0:T(8,128)(2,1)S(1)} %shard_map.90), channel_id=1, replica_groups={{0,4,8,12,16,20,24,28,32,36,40,44},{2,6,10,14,18,22,26,30,34,38,42,46},..., dimensions={0} | all-to-all | bytes 147456 | tf_op jit(solution)/shard_map/all_to_all | solution.py:328
  108.1 0.7 shard_map.91
  108.8 4.4 %all-to-all-start.3 = ((bf16[24,24,128]{2,1,0:T(8,128)(2,1)}), bf16[24,24,128]{2,1,0:T(8,128)(2,1)S(1)}, u32[]{:S(2)}, u32[]{:S(2)}) async-start(bf16[24,24,128]{2,1,0:T(8,128)(2,1)} %shard_map.91), calls=%async_computation.3 | async-start | bytes 294912 | tf_op jit(solution)/shard_map/all_to_all | solution.py:336
  113.2 2.1 %collective-permute-start.6 = (bf16[640,128]{1,0:T(8,128)(2,1)S(1)}, bf16[640,128]{1,0:T(8,128)(2,1)S(1)}, u32[]{:S(2)}, u32[]{:S(2)}) collective-permute-start(bf16[640,128]{1,0:T(8,128)(2,1)S(1)} %get-tuple-element.14), channel_id=1, source_target_pairs={{0,2},{1,3},{2,0},{3,1},{4,6},{5,7},{6,4},{7,5},{8,10},{9,11},{10,... | collective-permute-start | bytes 491528 | tf_op jit(solution)/shard_map/ppermute | solution.py:32
  115.3 5.5 %collective-permute-done.6.received = bf16[640,128]{1,0:T(8,128)(2,1)S(1)} collective-permute-done((bf16[640,128]{1,0:T(8,128)(2,1)S(1)}, bf16[640,128]{1,0:T(8,128)(2,1)S(1)}, u32[]{:S(2)}, u32[]{:S(2)}) %collective-permute-start.6) | collective-permute-done | bytes 163872 | tf_op jit(solution)/shard_map/ppermute | solution.py:32
  120.8 1.9 %copy-done = bf16[1280,1280]{1,0:T(8,128)(2,1)S(1)} copy-done((bf16[1280,1280]{1,0:T(8,128)(2,1)S(1)}, bf16[1280,1280]{1,0:T(8,128)(2,1)}, u32[]{:S(2)}) %copy-start) | copy-done | bytes 3276824
  122.7 1.9 %shard_map.88 = bf16[128,1280]{1,0:T(8,128)(2,1)} custom-call(s32[1]{0:T(128)} %bitcast.place, bf16[640,256]{1,0:T(8,128)(2,1)S(1)} %copy-done.2, bf16[640,128]{1,0:T(8,128)(2,1)S(1)} %collective-permute-done.6.received, bf16[1280,1280]{1,0:T(8,128)(2,1)S(1)} %copy-done, bf16[128,1280]{1,0:T(8,128)(2,1)S(1)} %bitcast.8), custom_call_target="tpu_custom_call" | custom-call | flops 419430400 | bytes 3276800 | tf_op jit(solution)/shard_map/pallas_call | solution.py:305
  124.6 0.7 shard_map.92
  (15 shorter events, 0.0 us)
Async XLA Ops:
  3.7 20.7 %collective-permute-start.1 = (bf16[2,128,640]{2,1,0:T(8,128)(2,1)}, bf16[2,128,640]{2,1,0:T(8,128)(2,1)S(1)}, u32[]{:S(2)}, u32[]{:S(2)}) collective-permute-start(bf16[2,128,640]{2,1,0:T(8,128)(2,1)} %get-tuple-element.12), channel_id=1, source_target_pairs={{0,2},{1,3},{2,0},{3,1},{4,6},{5,7},{6,4},{7,5},{8,10},{9,11},{10,... | collective-permute-start | bytes 983048 | tf_op jit(solution)/shard_map/ppermute | solution.py:32
  15.0 33.3 %all-to-all-start = ((bf16[4,640,128]{2,1,0:T(8,128)(2,1)}), bf16[4,640,128]{2,1,0:T(8,128)(2,1)S(1)}, u32[]{:S(2)}, u32[]{:S(2)}) async-start(bf16[4,640,128]{2,1,0:T(8,128)(2,1)} %get-tuple-element.15), calls=%async_computation | async-start | bytes 1310720 | tf_op jit(solution)/shard_map/all_to_all | solution.py:272
  18.5 19.2 %collective-permute-start.4 = (bf16[2,128,640]{2,1,0:T(8,128)(2,1)}, bf16[2,128,640]{2,1,0:T(8,128)(2,1)S(1)}, u32[]{:S(2)}, u32[]{:S(2)}) collective-permute-start(bf16[2,128,640]{2,1,0:T(8,128)(2,1)} %get-tuple-element.11.kv_own), channel_id=1, source_target_pairs={{4,0},{5,1},{6,2},{7,3},{8,4},{9,5},{10,6},{11,7},{12,8},{13,9},{1... | collective-permute-start | bytes 983048 | tf_op jit(solution)/shard_map/ppermute | solution.py:32
  19.8 17.9 %collective-permute-start.2 = (bf16[2,128,640]{2,1,0:T(8,128)(2,1)}, bf16[2,128,640]{2,1,0:T(8,128)(2,1)S(1)}, u32[]{:S(2)}, u32[]{:S(2)}) collective-permute-start(bf16[2,128,640]{2,1,0:T(8,128)(2,1)} %get-tuple-element.11.kv_own), channel_id=1, source_target_pairs={{0,4},{1,5},{2,6},{3,7},{4,8},{5,9},{6,10},{7,11},{8,12},{9,13},{1... | collective-permute-start | bytes 983048 | tf_op jit(solution)/shard_map/ppermute | solution.py:32
  24.4 13.3 %collective-permute-start.5 = (bf16[2,128,640]{2,1,0:T(8,128)(2,1)S(1)}, bf16[2,128,640]{2,1,0:T(8,128)(2,1)S(1)}, u32[]{:S(2)}, u32[]{:S(2)}) collective-permute-start(bf16[2,128,640]{2,1,0:T(8,128)(2,1)S(1)} %collective-permute-done.1.kv_pair), channel_id=1, source_target_pairs={{4,0},{5,1},{6,2},{7,3},{8,4},{9,5},{10,6},{11,7},{12,8},{13,9},{1... | collective-permute-start | bytes 983048 | tf_op jit(solution)/shard_map/ppermute | solution.py:32
  25.7 12.8 %collective-permute-start.3 = (bf16[2,128,640]{2,1,0:T(8,128)(2,1)S(1)}, bf16[2,128,640]{2,1,0:T(8,128)(2,1)S(1)}, u32[]{:S(2)}, u32[]{:S(2)}) collective-permute-start(bf16[2,128,640]{2,1,0:T(8,128)(2,1)S(1)} %collective-permute-done.1.kv_pair), channel_id=1, source_target_pairs={{0,4},{1,5},{2,6},{3,7},{4,8},{5,9},{6,10},{7,11},{8,12},{9,13},{1... | collective-permute-start | bytes 983048 | tf_op jit(solution)/shard_map/ppermute | solution.py:32
  30.3 7.4 %collective-permute-start = (bf16[128,640]{1,0:T(8,128)(2,1)}, bf16[128,640]{1,0:T(8,128)(2,1)S(1)}, u32[]{:S(2)}, u32[]{:S(2)}) collective-permute-start(bf16[128,640]{1,0:T(8,128)(2,1)} %get-tuple-element.10), channel_id=1, source_target_pairs={{0,2},{1,3},{2,0},{3,1},{4,6},{5,7},{6,4},{7,5},{8,10},{9,11},{10,... | collective-permute-start | bytes 491528 | tf_op jit(solution)/shard_map/ppermute | solution.py:32
  38.5 1.0 copy-start.4
  39.5 0.9 copy-start.5
  40.4 0.7 copy-start.6
  41.1 79.7 %copy-start.3 = (bf16[1,128,1280]{2,1,0:T(8,128)(2,1)S(1)}, bf16[1,128,1280]{2,1,0:T(8,128)(2,1)}, u32[]{:S(2)}) copy-start(bf16[1,128,1280]{2,1,0:T(8,128)(2,1)} %param.10) | copy-start | bytes 983044
  46.4 3.5 %copy-start.1 = (bf16[640,256]{1,0:T(8,128)(2,1)}, bf16[640,256]{1,0:T(8,128)(2,1)S(1)}, u32[]{:S(2)}) copy-start(bf16[640,256]{1,0:T(8,128)(2,1)S(1)} %get-tuple-element.13.attended.att) | copy-start | bytes 983044
  46.4 3.5 %collective-permute-start.7 = (bf16[640,256]{1,0:T(8,128)(2,1)S(1)}, bf16[640,256]{1,0:T(8,128)(2,1)S(1)}, u32[]{:S(2)}, u32[]{:S(2)}) collective-permute-start(bf16[640,256]{1,0:T(8,128)(2,1)S(1)} %get-tuple-element.13.attended.att), channel_id=1, source_target_pairs={{0,1},{1,0},{2,3},{3,2},{4,5},{5,4},{6,7},{7,6},{8,9},{9,8},{10,11... | collective-permute-start | bytes 983048 | tf_op jit(solution)/shard_map/ppermute | solution.py:32
  48.3 1.6 %copy-start.7 = (bf16[4,640,128]{2,1,0:T(8,128)(2,1)}, bf16[4,640,128]{2,1,0:T(8,128)(2,1)S(1)}, u32[]{:S(2)}) copy-start(bf16[4,640,128]{2,1,0:T(8,128)(2,1)S(1)} %all-to-all-done.exchanged) | copy-start | bytes 1966084
  49.9 0.7 copy-start.8
  53.5 67.3 %copy-start.2 = (bf16[640,256]{1,0:T(8,128)(2,1)S(1)}, bf16[640,256]{1,0:T(8,128)(2,1)}, u32[]{:S(2)}) copy-start(bf16[640,256]{1,0:T(8,128)(2,1)} %copy-done.1) | copy-start | bytes 983044
  108.8 15.8 %all-to-all-start.3 = ((bf16[24,24,128]{2,1,0:T(8,128)(2,1)}), bf16[24,24,128]{2,1,0:T(8,128)(2,1)S(1)}, u32[]{:S(2)}, u32[]{:S(2)}) async-start(bf16[24,24,128]{2,1,0:T(8,128)(2,1)} %shard_map.91), calls=%async_computation.3 | async-start | bytes 294912 | tf_op jit(solution)/shard_map/all_to_all | solution.py:336
  113.2 7.6 %collective-permute-start.6 = (bf16[640,128]{1,0:T(8,128)(2,1)S(1)}, bf16[640,128]{1,0:T(8,128)(2,1)S(1)}, u32[]{:S(2)}, u32[]{:S(2)}) collective-permute-start(bf16[640,128]{1,0:T(8,128)(2,1)S(1)} %get-tuple-element.14), channel_id=1, source_target_pairs={{0,2},{1,3},{2,0},{3,1},{4,6},{5,7},{6,4},{7,5},{8,10},{9,11},{10,... | collective-permute-start | bytes 491528 | tf_op jit(solution)/shard_map/ppermute | solution.py:32
  120.8 1.9 %copy-start = (bf16[1280,1280]{1,0:T(8,128)(2,1)S(1)}, bf16[1280,1280]{1,0:T(8,128)(2,1)}, u32[]{:S(2)}) copy-start(bf16[1280,1280]{1,0:T(8,128)(2,1)} %weight.1) | copy-start | bytes 9830404
